TPU v7x, 32 devices: a whole 2x2x4 slice. The times are simulated.
32 devices in a mesh: groups: 2 (over x), ctx: 16 (over z, y, core).
Axes of the slice: x: 2, y: 2, z: 4, core: 2. Of those that a mesh axis runs over, the one named last changes fastest.
Arguments:
- q_latent: bfloat16 [128, 1536], P(('groups', 'ctx')), parts along dimension 0, may hold values from -64 to 64
- q_gain: float32 [1536], replicated, may hold values from 0.1 to 1.9
- w_uq: bfloat16 [1536, 24576], P(None, 'ctx'), may hold values from -0.15625 to 0.15625
- w_uk: bfloat16 [128, 128, 512], P('ctx'), may hold values from -0.5 to 0.5
- w_uv: bfloat16 [128, 512, 128], P('ctx'), may hold values from -0.25 to 0.25
- w_o: bfloat16 [16384, 7168], P('ctx'), may hold values from -0.046875 to 0.046875
- latent_cache: bfloat16 [65536, 576], P(('groups', 'ctx')), parts along dimension 0, may hold values from -1024 to 1024
- kv_scales: float32 [65536, 4], P(('groups', 'ctx')), parts along dimension 0, may hold values from 0.5 to 2
- selected: int32 [128, 32], P(('groups', 'ctx')), parts along dimension 0, may hold values from 0 to 511, as said below
- counts: int32 [128], P(('groups', 'ctx')), parts along dimension 0, may hold values from 8 to 32
Outputs:
- attn_out: bfloat16 [128, 7168], P(('groups', 'ctx')), parts along dimension 0
There are 2 independent parts, one for each index of `groups`. A program takes and returns all parts, laid end to end along the dimension named above; an argument that names none is the same for every part. Nothing has to cross between parts.
Inputs may be any that keep to these rules, and one draw needn't show every extreme that they name: `selected`: each row lists 32 different block numbers. Over the rows 4 i to 4 i + 4 - 1 (the query tokens of one device) and their first counts entries, at most 8 different listed blocks lie in the range 32 j to 32 j + 31 for any j.
All inputs are finite; a program needn't handle non-finite values.
Results may differ from a plain program's by a relative error of at most 0.01.
The roundings to bfloat16 on the way count: a program that leaves them out, or rounds other values in their place, can miss the bound.
Values may be sent and summed in bfloat16 or wider, within the bound.
A program may use at most 128 MiB of HBM per device.

v0:
```python
import math

import jax
import jax.numpy as jnp
from jax import lax
from jax.sharding import PartitionSpec as P

BLK = 64


norm_eps = 1e-06
rope_base = 10000.0


def rotate_rotary(rotary, positions):
    half_width = rotary.shape[-1] // 2
    freq_index = jnp.arange(half_width, dtype=jnp.float32)
    inverse_freq = jnp.exp(freq_index * (-2.0 * math.log(rope_base) / rotary.shape[-1]))
    angles = positions[:, None] * inverse_freq[None, :]
    cosine = jnp.cos(angles)[:, None, :]
    sine = jnp.sin(angles)[:, None, :]
    first_half = rotary[:, :, :half_width]
    second_half = rotary[:, :, half_width:]
    return jnp.concatenate(
        [first_half * cosine - second_half * sine, first_half * sine + second_half * cosine], axis=2
    )


def local(q_latent, q_gain, w_uq, w_uk, w_uv, w_o, latent_cache, kv_scales, selected, counts):
    n_devices = lax.axis_size("ctx")
    heads_local = w_uk.shape[0]
    width_content = w_uk.shape[1]
    width_latent = w_uk.shape[2]
    width_rotary = latent_cache.shape[1] - width_latent
    width_row = width_latent + width_rotary
    q_local = q_latent.shape[0]
    top_blocks = selected.shape[1]
    block_len = BLK
    blocks_local = latent_cache.shape[0] // block_len
    blocks_total = blocks_local * n_devices
    capacity = max(2, 4 * top_blocks // n_devices)
    latent_f = q_latent.astype(jnp.float32)
    normed = (
        latent_f
        * lax.rsqrt(jnp.mean(latent_f * latent_f, axis=1, keepdims=True) + norm_eps)
        * q_gain
    ).astype(jnp.bfloat16)
    scaled = (
        latent_cache[:, :width_latent].astype(jnp.float32)
        * jnp.repeat(kv_scales, width_latent // kv_scales.shape[1], axis=1)
    ).astype(jnp.bfloat16)
    cache_blocks = jnp.concatenate([scaled, latent_cache[:, width_latent:]], axis=1).reshape(
        blocks_local, block_len, width_row
    )
    live_sel = jnp.arange(top_blocks, dtype=jnp.int32)[None, :] < counts[:, None]
    block_match = selected[:, :, None] == jnp.arange(blocks_total, dtype=jnp.int32)[None, None, :]
    needed = (
        jnp.any(block_match & live_sel[:, :, None], axis=(0, 1))
        .reshape(n_devices, blocks_local)
        .astype(jnp.int32)
    )
    order_rank = jnp.cumsum(needed, axis=1) - 1
    slot_match = (needed[:, :, None] == 1) & (
        order_rank[:, :, None] == jnp.arange(capacity, dtype=jnp.int32)[None, None, :]
    )
    requests = jnp.sum(
        jnp.where(slot_match, jnp.arange(blocks_local, dtype=jnp.int32)[None, :, None], 0), axis=1
    )
    rank_flat = order_rank.reshape(blocks_total)
    sel_rank = jnp.sum(jnp.where(block_match, rank_flat[None, None, :], 0), axis=2)
    slot_index = jnp.where(live_sel, selected // blocks_local * capacity + sel_rank, 0)
    shard_piece = lax.all_gather(normed, "ctx", axis=0, tiled=True)
    row_count = shard_piece.shape[0]
    projected = jnp.dot(shard_piece, w_uq, preferred_element_type=jnp.float32).reshape(
        row_count, heads_local, width_content + width_rotary
    )
    content = projected[:, :, :width_content].astype(jnp.bfloat16)
    positions = jnp.arange(row_count, dtype=jnp.int32).astype(jnp.float32)
    rotated = rotate_rotary(projected[:, :, width_content:], positions).astype(jnp.bfloat16)
    absorbed = jnp.einsum("khn,hnc->khc", content, w_uk, preferred_element_type=jnp.float32).astype(
        jnp.bfloat16
    )
    head_queries = jnp.concatenate([absorbed, rotated], axis=2)
    queries = lax.all_to_all(head_queries, "ctx", split_axis=0, concat_axis=1, tiled=True)
    served = cache_blocks[lax.all_to_all(requests, "ctx", split_axis=0, concat_axis=0, tiled=True)]
    fetched = lax.all_to_all(served, "ctx", split_axis=0, concat_axis=0, tiled=True)
    fetched_rows = fetched.reshape(n_devices * capacity * block_len, width_row)
    token_index = (
        slot_index[:, :, None] * block_len + jnp.arange(block_len, dtype=jnp.int32)[None, None, :]
    ).reshape(q_local, top_blocks * block_len)
    live_tokens = jnp.repeat(live_sel, block_len, axis=1)
    softmax_scale = 1.0 / math.sqrt(width_content + width_rotary)

    def attend(inputs):
        query_row, token_rows, live_row = inputs
        key_rows = fetched_rows[token_rows]
        scores = jnp.dot(query_row, key_rows.T, preferred_element_type=jnp.float32) * softmax_scale
        scores = jnp.where(live_row[None, :], scores, -jnp.inf)
        row_peak = jnp.max(scores, axis=1, keepdims=True)
        exponent = jnp.exp(scores - row_peak)
        weights = (exponent / jnp.sum(exponent, axis=1, keepdims=True)).astype(jnp.bfloat16)
        return jnp.dot(
            weights, key_rows[:, :width_latent], preferred_element_type=jnp.float32
        ).astype(jnp.bfloat16)

    latent_out = lax.map(attend, (queries, token_index, live_tokens))
    head_out = lax.all_to_all(latent_out, "ctx", split_axis=1, concat_axis=0, tiled=True)
    head_values = jnp.einsum(
        "qhc,hcv->qhv", head_out, w_uv, preferred_element_type=jnp.float32
    ).astype(jnp.bfloat16)
    head_values = head_values.reshape(head_values.shape[0], heads_local * w_uv.shape[2])
    return lax.psum_scatter(
        jnp.dot(head_values, w_o, preferred_element_type=jnp.float32),
        "ctx",
        scatter_dimension=0,
        tiled=True,
    ).astype(jnp.bfloat16)


def solution(mesh):
    in_specs = (
        P(("groups", "ctx"), None),
        P(),
        P(None, "ctx"),
        P("ctx", None, None),
        P("ctx", None, None),
        P("ctx", None),
        P(("groups", "ctx"), None),
        P(("groups", "ctx"), None),
        P(("groups", "ctx"), None),
        P(("groups", "ctx")),
    )
    out_specs = P(("groups", "ctx"), None)
    return jax.shard_map(local, mesh=mesh, in_specs=in_specs, out_specs=out_specs, check_vma=False)
```

profile of v0, /device:TPU:0, one launch (start us, length us, event | category | flops | bytes accessed | tf_op | source)
XLA Modules:
  0.0 466.6 jit_solution(13454047989507777395)
XLA Ops:
  0.0 0.8 iota_compare_fusion.2
  0.8 0.8 fusion.22
  1.9 1.0 select_reduce_fusion.1
  2.9 7.4 %all-to-all-start.1 = ((s32[16,1,8]{2,1,0:T(1,128)}), s32[16,1,8]{2,1,0:T(1,128)S(1)}, u32[]{:S(2)}, u32[]{:S(2)}) async-start(s32[16,1,8]{2,1,0:T(1,128)} %bitcast.18), calls=%async_computation.1 | async-start | bytes 16384 | tf_op jit(solution)/shard_map/all_to_all | solution.py:85
  10.3 0.8 fusion.27
  11.2 0.8 fusion.30
  12.0 22.2 %all-gather = bf16[16,4,1536]{2,1,0:T(4,128)(2,1)S(1)} all-gather(bf16[1,4,1536]{2,1,0:T(4,128)(2,1)S(1)} %fusion.30), channel_id=1, replica_groups=mesh['groups'=2,'ctx'=16] {'ctx'}, dimensions={0}, use_global_device_ids=true | all-gather | bytes 208896 | tf_op jit(solution)/shard_map/all_gather | solution.py:72
  34.2 3.3 fusion.39
  38.0 0.3 fusion.19
  38.6 1.2 copy.45
  39.8 0.4 copy.48
  40.2 0.2 slice-done
  40.4 2.5 copy.59
  42.9 1.0 copy.60
  44.0 4.3 all-to-all-start
  48.2 4.7 %broadcast_in_dim.79 = f32[2048,4,128]{2,1,0:T(4,128)S(1)} broadcast(f32[2048,4]{1,0:T(8,128)S(1)} %copy.48), dimensions={0,1} | broadcast | bytes 4227072 | tf_op jit(solution)/shard_map/broadcast_in_dim | solution.py:50
  52.9 1.0 fusion.18
  54.0 0.2 pad_maximum_fusion
  54.5 7.7 %gather_fusion.1 = bf16[128,64,576]{2,1,0:T(8,128)(2,1)} fusion(bf16[32,64,576]{2,1,0:T(8,128)(2,1)S(1)} %bitcast.67, s32[1024]{0:T(1024)S(1)} %pad_clamp_fusion), kind=kCustom, calls=%fused_computation.1 | custom fusion | bytes 18874880 | tf_op jit(solution)/shard_map/gather | solution.py:85
  62.1 2.7 all-to-all-done
  64.8 5.1 %all-to-all-start.2 = ((bf16[16,8,64,576]{3,2,1,0:T(8,128)(2,1)}), bf16[16,8,64,576]{3,2,1,0:T(8,128)(2,1)}, u32[]{:S(2)}, u32[]{:S(2)}) async-start(bf16[16,8,64,576]{3,2,1,0:T(8,128)(2,1)} %bitcast.68), calls=%async_computation.2 | async-start | bytes 20971520 | tf_op jit(solution)/shard_map/all_to_all | solution.py:86
  70.8 1.1 copy.79
  72.0 184.8 %all-to-all-done.2 = bf16[16,8,64,576]{3,2,1,0:T(8,128)(2,1)} async-done(((bf16[16,8,64,576]{3,2,1,0:T(8,128)(2,1)}), bf16[16,8,64,576]{3,2,1,0:T(8,128)(2,1)}, u32[]{:S(2)}, u32[]{:S(2)}) %all-to-all-start.2) | async-done | bytes 9437216 | tf_op jit(solution)/shard_map/all_to_all | solution.py:86
  256.8 63.6 %while.10 = (s32[]{:T(128)}, bf16[4,128,512]{2,1,0:T(8,128)(2,1)}, pred[4,2048]{1,0:T(4,128)(4,1)S(1)}, bf16[4,128,576]{2,1,0:T(8,128)(2,1)S(1)}, s32[4,2048]{1,...) while((s32[]{:T(128)}, bf16[4,128,512]{2,1,0:T(8,128)(2,1)}, pred[4,2048]{1,0:T(4,128)(4,1)S(1)}, ...), condition=%wide.region_8.9_spmd, body=%wide.region_5.8_spmd.sunk | while | flops 572595968 | bytes 12928089 | solution.py:106
  256.8 13.3 %gather_fusion = bf16[2048,576]{1,0:T(8,128)(2,1)S(1)} fusion(bf16[8192,576]{1,0:T(8,128)(2,1)} %get-tuple-element.118, s32[2048]{0:T(1024)S(1)} %broadcast_clamp_fusion.2), kind=kCustom, calls=%fused_computation.clone.1 | custom fusion | bytes 4726784 | tf_op jit(solution)/shard_map/while/body/eval_jaxpr/gather | solution.py:96
  270.2 1.1 fusion.54
  271.2 0.3 fusion.55
  271.5 1.2 fusion.56
  272.8 13.3 %gather_fusion = bf16[2048,576]{1,0:T(8,128)(2,1)S(1)} fusion(bf16[8192,576]{1,0:T(8,128)(2,1)} %get-tuple-element.118, s32[2048]{0:T(1024)S(1)} %broadcast_clamp_fusion.2), kind=kCustom, calls=%fused_computation.clone.1 | custom fusion | bytes 4726784 | tf_op jit(solution)/shard_map/while/body/eval_jaxpr/gather | solution.py:96
  286.1 1.1 fusion.54
  287.2 0.3 fusion.55
  287.5 1.2 fusion.56
  288.7 13.3 %gather_fusion = bf16[2048,576]{1,0:T(8,128)(2,1)S(1)} fusion(bf16[8192,576]{1,0:T(8,128)(2,1)} %get-tuple-element.118, s32[2048]{0:T(1024)S(1)} %broadcast_clamp_fusion.2), kind=kCustom, calls=%fused_computation.clone.1 | custom fusion | bytes 4726784 | tf_op jit(solution)/shard_map/while/body/eval_jaxpr/gather | solution.py:96
  302.0 1.1 fusion.54
  303.1 0.3 fusion.55
  303.4 1.2 fusion.56
  304.6 13.3 %gather_fusion = bf16[2048,576]{1,0:T(8,128)(2,1)S(1)} fusion(bf16[8192,576]{1,0:T(8,128)(2,1)} %get-tuple-element.118, s32[2048]{0:T(1024)S(1)} %broadcast_clamp_fusion.2), kind=kCustom, calls=%fused_computation.clone.1 | custom fusion | bytes 4726784 | tf_op jit(solution)/shard_map/while/body/eval_jaxpr/gather | solution.py:96
  317.9 1.1 fusion.54
  319.0 0.3 fusion.55
  319.3 1.2 fusion.56
  320.4 2.3 copy.54
  322.8 45.6 %all-to-all-start.3 = ((bf16[4,128,512]{2,0,1:T(4,128)(2,1)}), bf16[4,128,512]{2,0,1:T(4,128)(2,1)S(1)}, u32[]{:S(2)}, u32[]{:S(2)}) async-start(bf16[4,128,512]{2,0,1:T(4,128)(2,1)} %copy.54), calls=%async_computation.3 | async-start | bytes 1048576 | tf_op jit(solution)/shard_map/all_to_all | solution.py:107
  368.4 0.6 dynamic-slice
  369.7 13.0 %all-to-all-done.3 = bf16[4,128,512]{2,0,1:T(4,128)(2,1)S(1)} async-done(((bf16[4,128,512]{2,0,1:T(4,128)(2,1)}), bf16[4,128,512]{2,0,1:T(4,128)(2,1)S(1)}, u32[]{:S(2)}, u32[]{:S(2)}) %all-to-all-start.3) | async-done | bytes 524320 | tf_op jit(solution)/shard_map/all_to_all | solution.py:107
  383.0 0.3 fusion.20
  383.3 8.0 %fusion.23 = f32[64,7168]{1,0:T(8,128)S(1)} fusion(bf16[1024,7168]{1,0:T(8,128)(2,1)} %param.17, bf16[8,8,8,128]{3,2,1,0:T(8,128)(2,1)S(1)} %fusion.20), kind=kOutput, calls=%fused_computation.37 | convolution fusion | flops 939524096 | bytes 16646144 | tf_op jit(solution)/shard_map/dot_general | solution.py:113
  391.3 73.7 %all-reduce.2 = bf16[64,7168]{1,0:T(8,128)(2,1)} all-reduce(f32[64,7168]{1,0:T(8,128)S(1)} %fusion.23), channel_id=2, replica_groups=mesh['groups'=2,'ctx'=16] {'ctx'}, use_global_device_ids=true, to_apply=%region_9.10.clone | all-reduce | flops 458752 | bytes 2752512
  465.1 1.6 dynamic-slice_convert_fusion
  (67 shorter events, 2.8 us)
Async XLA Ops:
  0.0 38.0 %copy-start = (bf16[8,128,512]{2,1,0:T(8,128)(2,1)S(1)}, bf16[8,128,512]{2,1,0:T(8,128)(2,1)}, u32[]{:S(2)}) copy-start(bf16[8,128,512]{2,1,0:T(8,128)(2,1)} %param.15) | copy-start | bytes 3145732
  2.9 41.1 %all-to-all-start.1 = ((s32[16,1,8]{2,1,0:T(1,128)}), s32[16,1,8]{2,1,0:T(1,128)S(1)}, u32[]{:S(2)}, u32[]{:S(2)}) async-start(s32[16,1,8]{2,1,0:T(1,128)} %bitcast.18), calls=%async_computation.1 | async-start | bytes 16384 | tf_op jit(solution)/shard_map/all_to_all | solution.py:85
  38.6 1.2 copy-start.5
  38.6 1.8 slice-start
  39.8 3.1 slice-start.1
  44.0 20.9 %all-to-all-start = ((bf16[64,8,576]{2,1,0:T(8,128)(2,1)}), bf16[64,8,576]{2,1,0:T(8,128)(2,1)}, u32[]{:S(2)}, u32[]{:S(2)}) async-start(bf16[64,8,576]{2,1,0:T(8,128)(2,1)} %copy.45), calls=%async_computation | async-start | bytes 1310720 | tf_op jit(solution)/shard_map/all_to_all | solution.py:84
  48.2 4.7 %copy-start.2 = (bf16[2048,512]{1,0:T(8,128)(2,1)S(1)}, bf16[2048,512]{1,0:T(8,128)(2,1)}, u32[]{:S(2)}) copy-start(bf16[2048,512]{1,0:T(8,128)(2,1)} %copy.59) | copy-start | bytes 6291460
  52.9 1.0 copy-start.3
  64.8 5.2 %copy-start.6 = (s32[4,32]{1,0:T(4,128)S(1)}, s32[4,32]{1,0:T(4,128)}, u32[]{:S(2)}) copy-start(s32[4,32]{1,0:T(4,128)} %param.20) | copy-start | bytes 1540
  64.8 5.5 %copy-start.7 = (s32[4]{0:T(128)S(1)}, s32[4]{0:T(128)}, u32[]{:S(2)}) copy-start(s32[4]{0:T(128)} %param.21) | copy-start | bytes 52
  64.8 192.0 %all-to-all-start.2 = ((bf16[16,8,64,576]{3,2,1,0:T(8,128)(2,1)}), bf16[16,8,64,576]{3,2,1,0:T(8,128)(2,1)}, u32[]{:S(2)}, u32[]{:S(2)}) async-start(bf16[16,8,64,576]{3,2,1,0:T(8,128)(2,1)} %bitcast.68), calls=%async_computation.2 | async-start | bytes 20971520 | tf_op jit(solution)/shard_map/all_to_all | solution.py:86
  256.8 111.6 %copy-start.8 = (u32[32]{0:T(128)S(1)}, u32[32]{0:T(128)}, u32[]{:S(2)}) copy-start(u32[32]{0:T(128)} %constant.72) | copy-start | bytes 388
  320.4 62.6 %copy-start.4 = (bf16[8,512,128]{2,1,0:T(8,128)(2,1)S(1)}, bf16[8,512,128]{2,1,0:T(8,128)(2,1)}, u32[]{:S(2)}) copy-start(bf16[8,512,128]{2,1,0:T(8,128)(2,1)} %param.16) | copy-start | bytes 3145732
  322.8 59.9 %all-to-all-start.3 = ((bf16[4,128,512]{2,0,1:T(4,128)(2,1)}), bf16[4,128,512]{2,0,1:T(4,128)(2,1)S(1)}, u32[]{:S(2)}, u32[]{:S(2)}) async-start(bf16[4,128,512]{2,0,1:T(4,128)(2,1)} %copy.54), calls=%async_computation.3 | async-start | bytes 1048576 | tf_op jit(solution)/shard_map/all_to_all | solution.py:107
  383.3 83.3 %copy-start.1 = (bf16[8,128,512]{2,1,0:T(8,128)(2,1)S(1)}, bf16[8,128,512]{2,1,0:T(8,128)(2,1)}, u32[]{:S(2)}) copy-start(bf16[8,128,512]{2,1,0:T(8,128)(2,1)} %param.15) | copy-start | bytes 3145732
where the time goes:
time: 468 us; the launch traced here: 467 us
  waiting for transfers between devices  201 us (43%)
  blocking collectives  95.9 us (20%)
  local copies, waits for them, and re-layouts  78.1 us (17%)
  starting transfers between devices  62.5 us (13%)
  matrix products  20.8 us (4%)
  other arithmetic  7.66 us (2%)
    all_to_all x1, waiting for transfers between devices, local(): lax.all_to_all(served, 'ctx', split_axis=0, concat_axis=0, tiled=True)  185 us
    unnamed x1, blocking collectives  73.7 us
    gather x4, local copies, waits for them, and re-layouts, attend(): key_rows = fetched_rows[token_rows]  53.1 us
    all_to_all x1, starting transfers between devices, local(): lax.all_to_all(latent_out, 'ctx', split_axis=1, concat_axis=0, tiled=True)  45.6 us
    all_gather x1, blocking collectives, local(): shard_piece = lax.all_gather(normed, 'ctx', axis=0, tiled=True)  22.2 us
    all_to_all x1, waiting for transfers between devices, local(): lax.all_to_all(latent_out, 'ctx', split_axis=1, concat_axis=0, tiled=True)  13 us
  transfers between devices with their start and end apart: 4, of which 3 were waited for; matrix products, arithmetic and copies ran while one was open for 6% of the time, Pallas kernels for 0%

commit v1 on v0

v1 whole, which is shorter than its diff:
```python
import functools
import math

import jax
import jax.numpy as jnp
from jax import lax
from jax.experimental import pallas as pl
from jax.experimental.pallas import tpu as pltpu
from jax.sharding import PartitionSpec as P

BLK = 64
STEP = 4

norm_eps = 1e-06
rope_base = 10000.0
EMPTY = -1e30


def rotate_rotary(rotary, positions):
    half_width = rotary.shape[-1] // 2
    freq_index = jnp.arange(half_width, dtype=jnp.float32)
    inverse_freq = jnp.exp(freq_index * (-2.0 * math.log(rope_base) / rotary.shape[-1]))
    angles = positions[:, None] * inverse_freq[None, :]
    cosine = jnp.cos(angles)[:, None, :]
    sine = jnp.sin(angles)[:, None, :]
    first_half = rotary[:, :, :half_width]
    second_half = rotary[:, :, half_width:]
    return jnp.concatenate(
        [first_half * cosine - second_half * sine, first_half * sine + second_half * cosine], axis=2
    )


def xor_permute(value, n_devices, distance):
    return lax.ppermute(value, "ctx", [(i, i ^ distance) for i in range(n_devices)])


def masks_of(bits):
    out = [0]
    for bit in bits:
        out += [o | bit for o in out]
    return out


def attend_kernel(
    n_parts, n_chunks, width_latent, heads, scale, steps_ref, list_ref, *refs
):
    cache_in = refs[:n_parts]
    q_refs = refs[n_parts : n_parts + n_chunks]
    o_refs = refs[n_parts + n_chunks : n_parts + 2 * n_chunks]
    lse_ref, keys, acc, sems = refs[n_parts + 2 * n_chunks :]
    part_blocks = cache_in[0].shape[0]
    copies = [
        pltpu.make_async_copy(
            cache_in[i], keys.at[pl.ds(i * part_blocks, part_blocks)], sems.at[i]
        )
        for i in range(n_parts)
    ]
    for copy in copies:
        copy.start()
    groups, rows_chunk, _ = q_refs[0].shape
    rows = rows_chunk * n_chunks
    tokens = rows_chunk // heads
    span = STEP * BLK
    token_of_row = (lax.broadcasted_iota(jnp.int32, (rows, 1), 0) // heads) % tokens
    row_bit = lax.shift_left(jnp.ones_like(token_of_row), token_of_row)
    block_of_col = lax.broadcasted_iota(jnp.int32, (1, span), 1) // BLK
    diagonal = lax.broadcasted_iota(jnp.int32, (rows, rows), 0) == lax.broadcasted_iota(
        jnp.int32, (rows, rows), 1
    )
    for copy in copies:
        copy.wait()
    base = 2**tokens

    def group(g, carry):
        query = jnp.concatenate([q[g] for q in q_refs], axis=0)
        acc[...] = jnp.zeros_like(acc)

        def step(s, state):
            peak, total = state
            entries = [list_ref[g, s * STEP + k] for k in range(STEP)]
            key_rows = jnp.concatenate([keys[e // base] for e in entries], axis=0)
            bits = jnp.zeros((1, span), jnp.int32)
            for k in range(STEP):
                bits = jnp.where(block_of_col == k, entries[k] % base, bits)
            live = (bits & row_bit) != 0
            scores = (
                lax.dot_general(
                    query, key_rows, (((1,), (1,)), ((), ())), preferred_element_type=jnp.float32
                )
                * scale
            )
            scores = jnp.where(live, scores, EMPTY)
            new_peak = jnp.maximum(peak, jnp.max(scores, axis=1, keepdims=True))
            fade = jnp.exp(peak - new_peak)
            exponent = jnp.where(live, jnp.exp(scores - new_peak), 0.0)
            acc[...] = acc[...] * fade + jnp.dot(
                exponent.astype(jnp.bfloat16),
                key_rows[:, :width_latent],
                preferred_element_type=jnp.float32,
            )
            return new_peak, total * fade + jnp.sum(exponent, axis=1, keepdims=True)

        peak, total = lax.fori_loop(
            0,
            steps_ref[g],
            step,
            (jnp.full((rows, 1), EMPTY, jnp.float32), jnp.zeros((rows, 1), jnp.float32)),
        )
        some = total > 0.0
        safe = jnp.where(some, total, 1.0)
        out = (acc[...] / safe).astype(jnp.bfloat16)
        for j in range(n_chunks):
            o_refs[j][g] = out[j * rows_chunk : (j + 1) * rows_chunk]
        lse = jnp.where(some, peak + jnp.log(safe), EMPTY)
        lse_ref[pl.ds(g, 1), :] = jnp.sum(
            jnp.where(diagonal, lse, 0.0), axis=0, keepdims=True
        )
        return carry

    lax.fori_loop(0, groups, group, 0)


def attend(parts, chunks, block_list, steps, heads, width_latent, scale):
    n_parts, n_chunks = len(parts), len(chunks)
    part_blocks, _, width_row = parts[0].shape
    groups, rows_chunk, _ = chunks[0].shape
    vmem = pl.BlockSpec(memory_space=pltpu.VMEM)
    smem = pl.BlockSpec(memory_space=pltpu.SMEM)
    out = pl.pallas_call(
        functools.partial(attend_kernel, n_parts, n_chunks, width_latent, heads, scale),
        out_shape=[jax.ShapeDtypeStruct((groups, rows_chunk, width_latent), jnp.bfloat16)] * n_chunks
        + [jax.ShapeDtypeStruct((groups, rows_chunk * n_chunks), jnp.float32)],
        in_specs=[smem, smem] + [pl.BlockSpec(memory_space=pl.ANY)] * n_parts + [vmem] * n_chunks,
        out_specs=[vmem] * (n_chunks + 1),
        scratch_shapes=[
            pltpu.VMEM((n_parts * part_blocks, BLK, width_row), jnp.bfloat16),
            pltpu.VMEM((rows_chunk * n_chunks, width_latent), jnp.float32),
            pltpu.SemaphoreType.DMA((n_parts,)),
        ],
        compiler_params=pltpu.CompilerParams(vmem_limit_bytes=48 * 2**20),
        name="attend",
    )(steps, block_list, *parts, *chunks)
    return out[:n_chunks], out[n_chunks]


def local(
    cache_bits, query_bits, q_latent, q_gain, w_uq, w_uk, w_uv, w_o, latent_cache, kv_scales, selected, counts
):
    n_devices = lax.axis_size("ctx")
    me = lax.axis_index("ctx")
    heads_local, width_content, width_latent = w_uk.shape
    width_row = latent_cache.shape[1]
    width_rotary = width_row - width_latent
    q_local, top_blocks = selected.shape
    blocks_local = latent_cache.shape[0] // BLK
    tiles = kv_scales.shape[1]
    cache_masks, query_masks = masks_of(cache_bits), masks_of(query_bits)
    n_parts = len(cache_masks)

    cache_t = latent_cache.T
    scaled_t = (
        cache_t[:width_latent].astype(jnp.float32).reshape(tiles, width_latent // tiles, -1)
        * kv_scales.T[:, None, :]
    ).astype(jnp.bfloat16)
    own_cache = (
        jnp.concatenate([scaled_t.reshape(width_latent, -1), cache_t[width_latent:]], axis=0)
        .T.reshape(blocks_local, BLK, width_row)
    )
    parts = [own_cache]
    for bit in reversed(cache_bits):
        parts = parts + [xor_permute(p, n_devices, bit) for p in parts]
    parts_masks = [0]
    for bit in reversed(cache_bits):
        parts_masks = parts_masks + [m | bit for m in parts_masks]

    latent_f = q_latent.astype(jnp.float32)
    normed = (
        latent_f
        * lax.rsqrt(jnp.mean(latent_f * latent_f, axis=1, keepdims=True) + norm_eps)
        * q_gain
    ).astype(jnp.bfloat16)
    live_sel = jnp.arange(top_blocks, dtype=jnp.int32)[None, :] < counts[:, None]
    owner = jnp.where(live_sel, selected // blocks_local, -1)
    packed = jnp.concatenate(
        [normed, owner.astype(jnp.bfloat16), (selected % blocks_local).astype(jnp.bfloat16)], axis=1
    )
    gathered = lax.all_gather(packed, "ctx", axis=0, tiled=True)
    row_count = gathered.shape[0]
    latent_width = normed.shape[1]
    all_normed = gathered[:, :latent_width]
    all_owner = gathered[:, latent_width : latent_width + top_blocks].astype(jnp.int32)
    all_inner = gathered[:, latent_width + top_blocks :].astype(jnp.int32)

    projected = jnp.dot(all_normed, w_uq, preferred_element_type=jnp.float32).reshape(
        row_count, heads_local, width_content + width_rotary
    )
    content = projected[:, :, :width_content].astype(jnp.bfloat16)
    positions = jnp.arange(row_count, dtype=jnp.int32).astype(jnp.float32)
    rotated = rotate_rotary(projected[:, :, width_content:], positions).astype(jnp.bfloat16)
    absorbed = jnp.einsum("khn,hnc->khc", content, w_uk, preferred_element_type=jnp.float32).astype(
        jnp.bfloat16
    )
    groups = row_count // q_local
    own_queries = jnp.concatenate([absorbed, rotated], axis=2).reshape(
        groups, q_local * heads_local, width_row
    )
    chunks = [own_queries]
    chunk_masks = [0]
    for bit in reversed(query_bits):
        chunks = chunks + [xor_permute(c, n_devices, bit) for c in chunks]
        chunk_masks = chunk_masks + [m | bit for m in chunk_masks]

    n_held = n_parts * blocks_local
    place = jnp.full_like(all_owner, -1)
    for i, mask in enumerate(parts_masks):
        place = jnp.where(all_owner == (me ^ mask), i * blocks_local + all_inner, place)
    held = jnp.arange(n_held, dtype=jnp.int32)
    member = jnp.any(
        place.reshape(groups, q_local, top_blocks)[:, :, :, None] == held[None, None, None, :], axis=2
    ).astype(jnp.int32)
    bits = jnp.sum(
        member * lax.shift_left(1, jnp.arange(q_local, dtype=jnp.int32))[None, :, None], axis=1
    )
    needed = (bits > 0).astype(jnp.int32)
    rank = jnp.cumsum(needed, axis=1) - needed
    entry = held[None, :] * 2**q_local + bits
    slot = (rank[:, :, None] == held[None, None, :]) & (needed[:, :, None] == 1)
    block_list = jnp.sum(jnp.where(slot, entry[:, :, None], 0), axis=1)
    steps = (jnp.sum(needed, axis=1) + STEP - 1) // STEP

    scale = 1.0 / math.sqrt(width_content + width_rotary)
    outs, lse = attend(parts, chunks, block_list, steps, heads_local, width_latent, scale)

    rows_chunk = q_local * heads_local
    values, logs = [], []
    for i, mask in enumerate(chunk_masks):
        part_lse = lse[:, i * rows_chunk : (i + 1) * rows_chunk]
        values.append(outs[i] if mask == 0 else xor_permute(outs[i], n_devices, mask))
        logs.append(part_lse if mask == 0 else xor_permute(part_lse, n_devices, mask))
    top = functools.reduce(jnp.maximum, logs)
    shares = [jnp.exp(x - top) for x in logs]
    total = functools.reduce(jnp.add, shares)
    latent_out = functools.reduce(
        jnp.add, [v.astype(jnp.float32) * (s / total)[:, :, None] for v, s in zip(values, shares)]
    ).astype(jnp.bfloat16)
    head_out = latent_out.reshape(row_count, heads_local, width_latent)
    head_values = jnp.einsum(
        "qhc,hcv->qhv", head_out, w_uv, preferred_element_type=jnp.float32
    ).astype(jnp.bfloat16)
    head_values = head_values.reshape(row_count, heads_local * w_uv.shape[2])
    result = jnp.dot(head_values, w_o, preferred_element_type=jnp.float32)

    result = result.reshape((2,) * (n_devices.bit_length() - 1) + (q_local, -1))
    axis = n_devices.bit_length() - 2
    bit = 1
    while bit < n_devices:
        mine = (me // bit) % 2
        keep = lax.dynamic_index_in_dim(result, mine, axis, keepdims=False)
        send = lax.dynamic_index_in_dim(result, 1 - mine, axis, keepdims=False)
        result = keep + xor_permute(send.astype(jnp.bfloat16), n_devices, bit).astype(jnp.float32)
        axis -= 1
        bit *= 2
    return result.astype(jnp.bfloat16)


def solution(mesh):
    n_devices = mesh.shape["ctx"]
    all_bits = [1 << i for i in range(n_devices.bit_length() - 1)]
    cache_bits, query_bits = all_bits[:2], all_bits[2:]
    in_specs = (
        P(("groups", "ctx"), None),
        P(),
        P(None, "ctx"),
        P("ctx", None, None),
        P("ctx", None, None),
        P("ctx", None),
        P(("groups", "ctx"), None),
        P(("groups", "ctx"), None),
        P(("groups", "ctx"), None),
        P(("groups", "ctx")),
    )
    out_specs = P(("groups", "ctx"), None)
    return jax.shard_map(
        functools.partial(local, cache_bits, query_bits),
        mesh=mesh,
        in_specs=in_specs,
        out_specs=out_specs,
        check_vma=False,
    )
```

time: 468 us -> 272 us (0.58)
  waiting for transfers between devices: 201 us -> 111 us
  local copies, waits for them, and re-layouts: 78.1 us -> 7.48 us
  starting transfers between devices: 62.5 us -> 9.95 us
  Pallas kernels: 0 us -> 43.5 us
  blocking collectives: 95.9 us -> 72.6 us
  matrix products: 20.8 us -> 12.2 us
    all_to_all x4 -> x0, waiting for transfers between devices: 201 us -> none  [the longest x1 185 us: local(): lax.all_to_all(served, 'ctx', split_axis=0, concat_axis=0, tiled=True)]
    ppermute x0 -> x16, waiting for transfers between devices: none -> 111 us  [xor_permute(): lax.ppermute(value, 'ctx', [(i, i ^ distance) for i in range(n_devices)])]
    unnamed x1 -> x0, blocking collectives: 73.7 us -> none
    all_to_all x4 -> x0, starting transfers between devices: 62.5 us -> none  [the longest x1 45.6 us: local(): lax.all_to_all(latent_out, 'ctx', split_axis=1, concat_axis=0, tiled=True)]
    gather x5 -> x0, local copies, waits for them, and re-layouts: 60.8 us -> none  [the longest x4 53.1 us: attend(): key_rows = fetched_rows[token_rows]]
    all_gather x1, blocking collectives: 22.2 us -> 72.6 us  [local(): gathered = lax.all_gather(packed, 'ctx', axis=0, tiled=True)]
    pallas_call x0 -> x1, Pallas kernels: none -> 43.5 us  [attend(): pl.pallas_call(functools.partial(attend_kernel, n_parts, n_chunks, width_...]
    ppermute x0 -> x16, starting transfers between devices: none -> 9.95 us  [xor_permute(): lax.ppermute(value, 'ctx', [(i, i ^ distance) for i in range(n_devices)])]
  transfers between devices with their start and end apart: 4 -> 16, of which waited for: 3 -> 8; matrix products, arithmetic and copies ran while one was open for 6% -> 3% of each run, Pallas kernels for 0% -> 0%
where the time goes in v1:
time: 272 us; the launch traced here: 267 us
  waiting for transfers between devices  111 us (41%)
  blocking collectives  72.6 us (27%)
  Pallas kernels  43.5 us (16%)
  matrix products  12.2 us (4%)
  starting transfers between devices  9.95 us (4%)
  other arithmetic  9.8 us (4%)
  local copies, waits for them, and re-layouts  7.48 us (3%)
    ppermute x16, waiting for transfers between devices, xor_permute(): lax.ppermute(value, 'ctx', [(i, i ^ distance) for i in range(n_devices)])  111 us
    all_gather x1, blocking collectives, local(): gathered = lax.all_gather(packed, 'ctx', axis=0, tiled=True)  72.6 us
    pallas_call x1, Pallas kernels, attend(): pl.pallas_call(functools.partial(attend_kernel, n_parts, n_chunks, width_...  43.5 us
    ppermute x16, starting transfers between devices, xor_permute(): lax.ppermute(value, 'ctx', [(i, i ^ distance) for i in range(n_devices)])  9.95 us
    dot_general x1, matrix products, local(): result = jnp.dot(head_values, w_o, preferred_element_type=jnp.float32)  8.28 us
  transfers between devices with their start and end apart: 16, of which 8 were waited for; matrix products, arithmetic and copies ran while one was open for 3% of the time, Pallas kernels for 0%

profile of v1, /device:TPU:0, one launch (start us, length us, event | category | flops | bytes accessed | tf_op | source)
XLA Modules:
  0.0 266.9 jit_solution(8756076232194061664)
XLA Ops:
  0.0 1.1 slice.55
  1.1 2.2 fusion.2
  3.2 0.2 maximum_bitcast_fusion
  3.5 2.6 copy.32
  6.1 3.0 %collective-permute-start = (bf16[32,64,576]{2,1,0:T(8,128)(2,1)}, bf16[32,64,576]{2,1,0:T(8,128)(2,1)}, u32[]{:S(2)}, u32[]{:S(2)}) collective-permute-start(bf16[32,64,576]{2,1,0:T(8,128)(2,1)} %bitcast.47), channel_id=1, source_target_pairs={{0,2},{1,3},{2,0},{3,1},{4,6},{5,7},{6,4},{7,5},{8,10},{9,11},{10,... | collective-permute-start | bytes 7077896 | tf_op jit(solution)/shard_map/ppermute | solution.py:34
  9.1 0.1 fusion.18
  9.4 0.1 concatenate.12
  9.5 72.6 %all-gather = bf16[16,4,1600]{2,1,0:T(4,128)(2,1)S(1)} all-gather(bf16[1,4,1600]{2,1,0:T(4,128)(2,1)S(1)} %bitcast.54), channel_id=1, replica_groups=mesh['groups'=2,'ctx'=16] {'ctx'}, dimensions={0}, use_global_device_ids=true | all-gather | bytes 217600 | tf_op jit(solution)/shard_map/all_gather | solution.py:187
  82.1 0.1 reshape.142
  82.2 0.7 copy-done.3
  82.9 3.3 %fusion.10 = f32[64,1536]{1,0:T(8,128)S(1)} fusion(bf16[1536,1536]{1,0:T(8,128)(2,1)} %param.12, bf16[64,1600]{1,0:T(8,128)(2,1)S(1)} %reshape.142), kind=kOutput, calls=%fused_computation.28 | convolution fusion | flops 301989888 | bytes 5308416 | tf_op jit(solution)/shard_map/dot_general | solution.py:194
  86.2 0.2 reshape.138
  86.4 0.2 multiply_cosine_fusion
  86.6 0.1 fusion.29
  86.7 0.4 collective-permute-start.2
  87.1 0.1 subtract_convert_fusion
  87.3 0.3 fusion.3
  87.6 0.1 pad_maximum_fusion
  87.7 0.4 copy.36
  88.2 0.9 fusion.15
  89.1 0.4 fusion.5
  89.5 0.1 select_reduce_fusion.1
  89.6 0.3 reduce_window_sum.11
  89.9 0.1 convert_subtract_fusion
  90.0 28.1 %collective-permute-done.3.refs_5_ = bf16[16,32,576]{2,1,0:T(8,128)(2,1)S(1)} collective-permute-done((bf16[16,32,576]{2,1,0:T(8,128)(2,1)S(1)}, bf16[16,32,576]{2,1,0:T(8,128)(2,1)S(1)}, u32[]{:S(2)}, u32[]{:S(2)}) %collective-permute-start.3) | collective-permute-done | bytes 589856 | tf_op jit(solution)/shard_map/ppermute | solution.py:34
  118.2 1.2 select_reduce_fusion.list_ref
  119.4 15.4 %collective-permute-done.5.refs_7_ = bf16[16,32,576]{2,1,0:T(8,128)(2,1)S(1)} collective-permute-done((bf16[16,32,576]{2,1,0:T(8,128)(2,1)S(1)}, bf16[16,32,576]{2,1,0:T(8,128)(2,1)S(1)}, u32[]{:S(2)}, u32[]{:S(2)}) %collective-permute-start.5) | collective-permute-done | bytes 589856 | tf_op jit(solution)/shard_map/ppermute | solution.py:34
  134.8 43.5 %attend.1 = (bf16[16,32,512]{2,1,0:T(8,128)(2,1)S(1)}, bf16[16,32,512]{2,1,0:T(8,128)(2,1)}, bf16[16,32,512]{2,1,0:T(8,128)(2,1)}, bf16[16,32,512]{2,1,0:T(8,128)(2,1)}, f32[16,128]{1,0:T(8,128)S(1)}) custom-call(s32[16]{0:T(128)S(1)} %and_select_fusion.steps_ref, s32[16,128]{1,0:T(8,128)S(1)} %select_reduce_fusion.list_ref, bf16[32,64,576]{2,1,0:T(8,128)(2,1)} %bitcast.49, ...), custom_call_target="tpu_custom_call" | custom-call | tf_op jit(solution)/shard_map/attend/pallas_call | solution.py:129
  178.4 1.0 collective-permute-start.11
  179.4 2.5 collective-permute-start.9
  182.0 0.4 collective-permute-start.6
  182.4 1.0 collective-permute-start.7
  183.4 43.5 %collective-permute-done.6 = f32[16,32]{1,0:T(8,128)S(1)} collective-permute-done((f32[16,32]{1,0:T(8,128)S(1)}, f32[16,32]{1,0:T(8,128)S(1)}, u32[]{:S(2)}, u32[]{:S(2)}) %collective-permute-start.6) | collective-permute-done | bytes 2080 | tf_op jit(solution)/shard_map/ppermute | solution.py:34
  226.9 1.2 collective-permute-start.8
  228.1 4.3 %collective-permute-done.8 = f32[16,32]{1,0:T(8,128)S(1)} collective-permute-done((f32[16,32]{1,0:T(8,128)S(1)}, f32[16,32]{1,0:T(8,128)S(1)}, u32[]{:S(2)}, u32[]{:S(2)}) %collective-permute-start.8) | collective-permute-done | bytes 2080 | tf_op jit(solution)/shard_map/ppermute | solution.py:34
  232.4 1.7 add_convert_fusion
  234.1 0.4 fusion.4
  234.5 0.1 copy.38
  234.7 8.3 %fusion = f32[2,2,2,2,4,7168]{5,4,3,2,1,0:T(4,128)S(1)} fusion(bf16[2,2,2,2,4,1024]{5,4,3,2,1,0:T(4,128)(2,1)S(1)} %dot_general.17, bf16[1024,7168]{1,0:T(8,128)(2,1)} %param.15), kind=kOutput, calls=%fused_computation | convolution fusion | flops 939524096 | bytes 16646144 | tf_op jit(solution)/shard_map/dot_general | solution.py:251
  243.0 0.9 fusion.8
  243.9 2.0 collective-permute-done.12
  245.9 0.2 bitcast_add_fusion
  246.2 0.9 copy-done.1
  247.3 7.6 %collective-permute-done.13 = bf16[2,2,4,7168]{3,2,1,0:T(4,128)(2,1)S(1)} collective-permute-done((bf16[2,2,4,7168]{3,2,1,0:T(4,128)(2,1)S(1)}, bf16[2,2,4,7168]{3,2,1,0:T(4,128)(2,1)S(1)}, u32[]{:S(2)}, u32[]{:S(2)}) %collective-permute-start.13) | collective-permute-done | bytes 229408 | tf_op jit(solution)/shard_map/ppermute | solution.py:34
  254.9 1.1 bitcast_add_fusion.1
  256.2 4.7 %collective-permute-done.14 = bf16[2,4,7168]{2,1,0:T(4,128)(2,1)S(1)} collective-permute-done((bf16[2,4,7168]{2,1,0:T(4,128)(2,1)S(1)}, bf16[2,4,7168]{2,1,0:T(4,128)(2,1)S(1)}, u32[]{:S(2)}, u32[]{:S(2)}) %collective-permute-start.14) | collective-permute-done | bytes 114720 | tf_op jit(solution)/shard_map/ppermute | solution.py:34
  261.1 5.1 %collective-permute-done.15 = bf16[4,7168]{1,0:T(4,128)(2,1)S(1)} collective-permute-done((bf16[4,7168]{1,0:T(4,128)(2,1)S(1)}, bf16[4,7168]{1,0:T(4,128)(2,1)S(1)}, u32[]{:S(2)}, u32[]{:S(2)}) %collective-permute-start.15) | collective-permute-done | bytes 57376 | tf_op jit(solution)/shard_map/ppermute | solution.py:34
  266.3 0.7 fusion.13
  (51 shorter events, 1.1 us)
Async XLA Ops:
  0.0 87.2 %copy-start = (bf16[8,128,512]{2,1,0:T(8,128)(2,1)S(1)}, bf16[8,128,512]{2,1,0:T(8,128)(2,1)}, u32[]{:S(2)}) copy-start(bf16[8,128,512]{2,1,0:T(8,128)(2,1)} %param.13) | copy-start | bytes 3145732
  3.4 5.7 %copy-start.4 = (bf16[4,1536]{1,0:T(4,128)(2,1)S(1)}, bf16[4,1536]{1,0:T(4,128)(2,1)}, u32[]{:S(2)}) copy-start(bf16[4,1536]{1,0:T(4,128)(2,1)} %param.10) | copy-start | bytes 36868
  3.4 5.8 %copy-start.6 = (s32[4,32]{1,0:T(4,128)S(1)}, s32[4,32]{1,0:T(4,128)}, u32[]{:S(2)}) copy-start(s32[4,32]{1,0:T(4,128)} %param.18) | copy-start | bytes 1540
  3.4 5.8 %copy-start.7 = (s32[4]{0:T(128)S(1)}, s32[4]{0:T(128)}, u32[]{:S(2)}) copy-start(s32[4]{0:T(128)} %param.19) | copy-start | bytes 52
  3.5 5.8 %copy-start.5 = (f32[1536]{0:T(1024)S(1)}, f32[1536]{0:T(1024)}, u32[]{:S(2)}) copy-start(f32[1536]{0:T(1024)} %param.11) | copy-start | bytes 18436
  6.1 80.6 %collective-permute-start = (bf16[32,64,576]{2,1,0:T(8,128)(2,1)}, bf16[32,64,576]{2,1,0:T(8,128)(2,1)}, u32[]{:S(2)}, u32[]{:S(2)}) collective-permute-start(bf16[32,64,576]{2,1,0:T(8,128)(2,1)} %bitcast.47), channel_id=1, source_target_pairs={{0,2},{1,3},{2,0},{3,1},{4,6},{5,7},{6,4},{7,5},{8,10},{9,11},{10,... | collective-permute-start | bytes 7077896 | tf_op jit(solution)/shard_map/ppermute | solution.py:34
  9.1 125.7 %collective-permute-start.1 = (bf16[32,64,576]{2,1,0:T(8,128)(2,1)}, bf16[32,64,576]{2,1,0:T(8,128)(2,1)}, u32[]{:S(2)}, u32[]{:S(2)}) collective-permute-start(bf16[32,64,576]{2,1,0:T(8,128)(2,1)} %bitcast.48), channel_id=1, source_target_pairs={{0,1},{1,0},{2,3},{3,2},{4,5},{5,4},{6,7},{7,6},{8,9},{9,8},{10,11... | collective-permute-start | bytes 7077896 | tf_op jit(solution)/shard_map/ppermute | solution.py:34
  82.2 0.7 copy-start.3
  86.7 48.1 %collective-permute-start.2 = (bf16[32,64,576]{2,1,0:T(8,128)(2,1)}, bf16[32,64,576]{2,1,0:T(8,128)(2,1)}, u32[]{:S(2)}, u32[]{:S(2)}) collective-permute-start(bf16[32,64,576]{2,1,0:T(8,128)(2,1)} %collective-permute-done.refs_1_), channel_id=1, source_target_pairs={{0,1},{1,0},{2,3},{3,2},{4,5},{5,4},{6,7},{7,6},{8,9},{9,8},{10,11... | collective-permute-start | bytes 7077896 | tf_op jit(solution)/shard_map/ppermute | solution.py:34
  88.1 30.1 %collective-permute-start.3 = (bf16[16,32,576]{2,1,0:T(8,128)(2,1)S(1)}, bf16[16,32,576]{2,1,0:T(8,128)(2,1)S(1)}, u32[]{:S(2)}, u32[]{:S(2)}) collective-permute-start(bf16[16,32,576]{2,1,0:T(8,128)(2,1)S(1)} %bitcast.44), channel_id=1, source_target_pairs={{0,8},{1,9},{2,10},{3,11},{4,12},{5,13},{6,14},{7,15},{8,0},{9,1},... | collective-permute-start | bytes 1769480 | tf_op jit(solution)/shard_map/ppermute | solution.py:34
  88.1 31.2 %collective-permute-start.4 = (bf16[16,32,576]{2,1,0:T(8,128)(2,1)S(1)}, bf16[16,32,576]{2,1,0:T(8,128)(2,1)S(1)}, u32[]{:S(2)}, u32[]{:S(2)}) collective-permute-start(bf16[16,32,576]{2,1,0:T(8,128)(2,1)S(1)} %bitcast.45), channel_id=1, source_target_pairs={{0,4},{1,5},{2,6},{3,7},{4,0},{5,1},{6,2},{7,3},{8,12},{9,13},{10,... | collective-permute-start | bytes 1769480 | tf_op jit(solution)/shard_map/ppermute | solution.py:34
  118.2 16.6 %collective-permute-start.5 = (bf16[16,32,576]{2,1,0:T(8,128)(2,1)S(1)}, bf16[16,32,576]{2,1,0:T(8,128)(2,1)S(1)}, u32[]{:S(2)}, u32[]{:S(2)}) collective-permute-start(bf16[16,32,576]{2,1,0:T(8,128)(2,1)S(1)} %collective-permute-done.3.refs_5_), channel_id=1, source_target_pairs={{0,4},{1,5},{2,6},{3,7},{4,0},{5,1},{6,2},{7,3},{8,12},{9,13},{10,... | collective-permute-start | bytes 1769480 | tf_op jit(solution)/shard_map/ppermute | solution.py:34
  178.3 55.8 %copy-start.2 = (bf16[8,512,128]{2,1,0:T(8,128)(2,1)S(1)}, bf16[8,512,128]{2,1,0:T(8,128)(2,1)}, u32[]{:S(2)}) copy-start(bf16[8,512,128]{2,1,0:T(8,128)(2,1)} %param.14) | copy-start | bytes 3145732
  178.3 54.1 %collective-permute-start.10 = (bf16[16,32,512]{2,1,0:T(8,128)(2,1)}, bf16[16,32,512]{2,1,0:T(8,128)(2,1)S(1)}, u32[]{:S(2)}, u32[]{:S(2)}) collective-permute-start(bf16[16,32,512]{2,1,0:T(8,128)(2,1)} %get-tuple-element.13), channel_id=1, source_target_pairs={{0,4},{1,5},{2,6},{3,7},{4,0},{5,1},{6,2},{7,3},{8,12},{9,13},{10,... | collective-permute-start | bytes 1572872 | tf_op jit(solution)/shard_map/ppermute | solution.py:34
  178.4 54.0 %collective-permute-start.11 = (bf16[16,32,512]{2,1,0:T(8,128)(2,1)}, bf16[16,32,512]{2,1,0:T(8,128)(2,1)}, u32[]{:S(2)}, u32[]{:S(2)}) collective-permute-start(bf16[16,32,512]{2,1,0:T(8,128)(2,1)} %get-tuple-element.14), channel_id=1, source_target_pairs={{0,12},{1,13},{2,14},{3,15},{4,8},{5,9},{6,10},{7,11},{8,4},{9,5},... | collective-permute-start | bytes 1572872 | tf_op jit(solution)/shard_map/ppermute | solution.py:34
  179.4 53.0 %collective-permute-start.9 = (bf16[16,32,512]{2,1,0:T(8,128)(2,1)}, bf16[16,32,512]{2,1,0:T(8,128)(2,1)}, u32[]{:S(2)}, u32[]{:S(2)}) collective-permute-start(bf16[16,32,512]{2,1,0:T(8,128)(2,1)} %get-tuple-element.12), channel_id=1, source_target_pairs={{0,8},{1,9},{2,10},{3,11},{4,12},{5,13},{6,14},{7,15},{8,0},{9,1},... | collective-permute-start | bytes 1572872 | tf_op jit(solution)/shard_map/ppermute | solution.py:34
  182.0 44.9 %collective-permute-start.6 = (f32[16,32]{1,0:T(8,128)S(1)}, f32[16,32]{1,0:T(8,128)S(1)}, u32[]{:S(2)}, u32[]{:S(2)}) collective-permute-start(f32[16,32]{1,0:T(8,128)S(1)} %get-tuple-element.27), channel_id=1, source_target_pairs={{0,8},{1,9},{2,10},{3,11},{4,12},{5,13},{6,14},{7,15},{8,0},{9,1},... | collective-permute-start | bytes 6152 | tf_op jit(solution)/shard_map/ppermute | solution.py:34
  182.4 45.7 %collective-permute-start.7 = (f32[16,32]{1,0:T(8,128)S(1)}, f32[16,32]{1,0:T(8,128)S(1)}, u32[]{:S(2)}, u32[]{:S(2)}) collective-permute-start(f32[16,32]{1,0:T(8,128)S(1)} %get-tuple-element.29), channel_id=1, source_target_pairs={{0,4},{1,5},{2,6},{3,7},{4,0},{5,1},{6,2},{7,3},{8,12},{9,13},{10,... | collective-permute-start | bytes 6152 | tf_op jit(solution)/shard_map/ppermute | solution.py:34
  226.9 5.4 %collective-permute-start.8 = (f32[16,32]{1,0:T(8,128)S(1)}, f32[16,32]{1,0:T(8,128)S(1)}, u32[]{:S(2)}, u32[]{:S(2)}) collective-permute-start(f32[16,32]{1,0:T(8,128)S(1)} %get-tuple-element.28), channel_id=1, source_target_pairs={{0,12},{1,13},{2,14},{3,15},{4,8},{5,9},{6,10},{7,11},{8,4},{9,5},... | collective-permute-start | bytes 6152 | tf_op jit(solution)/shard_map/ppermute | solution.py:34
  243.9 2.0 collective-permute-start.12
  246.2 0.9 copy-start.1
  247.2 7.7 %collective-permute-start.13 = (bf16[2,2,4,7168]{3,2,1,0:T(4,128)(2,1)S(1)}, bf16[2,2,4,7168]{3,2,1,0:T(4,128)(2,1)S(1)}, u32[]{:S(2)}, u32[]{:S(2)}) collective-permute-start(bf16[2,2,4,7168]{3,2,1,0:T(4,128)(2,1)S(1)} %fusion.9), channel_id=1, source_target_pairs={{0,2},{1,3},{2,0},{3,1},{4,6},{5,7},{6,4},{7,5},{8,10},{9,11},{10,... | collective-permute-start | bytes 688136 | tf_op jit(solution)/shard_map/ppermute | solution.py:34
  256.1 4.9 %collective-permute-start.14 = (bf16[2,4,7168]{2,1,0:T(4,128)(2,1)S(1)}, bf16[2,4,7168]{2,1,0:T(4,128)(2,1)S(1)}, u32[]{:S(2)}, u32[]{:S(2)}) collective-permute-start(bf16[2,4,7168]{2,1,0:T(4,128)(2,1)S(1)} %fusion.12), channel_id=1, source_target_pairs={{0,4},{1,5},{2,6},{3,7},{4,0},{5,1},{6,2},{7,3},{8,12},{9,13},{10,... | collective-permute-start | bytes 344072 | tf_op jit(solution)/shard_map/ppermute | solution.py:34
  261.1 5.2 %collective-permute-start.15 = (bf16[4,7168]{1,0:T(4,128)(2,1)S(1)}, bf16[4,7168]{1,0:T(4,128)(2,1)S(1)}, u32[]{:S(2)}, u32[]{:S(2)}) collective-permute-start(bf16[4,7168]{1,0:T(4,128)(2,1)S(1)} %fusion.14), channel_id=1, source_target_pairs={{0,8},{1,9},{2,10},{3,11},{4,12},{5,13},{6,14},{7,15},{8,0},{9,1},... | collective-permute-start | bytes 172040 | tf_op jit(solution)/shard_map/ppermute | solution.py:34

commit v2 on v1

--- a/solution.py
+++ b/solution.py
@@ -9,7 +9,9 @@
 from jax.sharding import PartitionSpec as P
 
 BLK = 64
-STEP = 4
+STEP = 8
+SIDE = 2
+SPLIT = 1
 
 norm_eps = 1e-06
 rope_base = 10000.0
@@ -41,8 +43,45 @@
     return out
 
 
+def gather_kernel(n_devices, own_ref, out_ref, send_sems, recv_sems):
+    me = lax.axis_index("ctx")
+    barrier = pltpu.get_barrier_semaphore()
+    for d in range(1, n_devices):
+        pl.semaphore_signal(barrier, inc=1, device_id={"ctx": (me + d) % n_devices})
+    pl.semaphore_wait(barrier, n_devices - 1)
+    copies = [
+        pltpu.make_async_remote_copy(
+            src_ref=own_ref,
+            dst_ref=out_ref.at[me],
+            send_sem=send_sems.at[d],
+            recv_sem=recv_sems.at[d],
+            device_id={"ctx": (me + d) % n_devices},
+        )
+        for d in range(1, n_devices)
+    ]
+    for copy in copies:
+        copy.start()
+    out_ref[me] = own_ref[...]
+    for copy in copies:
+        copy.wait()
+
+
+def gather_rows(own, n_devices):
+    vmem = pl.BlockSpec(memory_space=pltpu.VMEM)
+    out = pl.pallas_call(
+        functools.partial(gather_kernel, n_devices),
+        out_shape=jax.ShapeDtypeStruct((n_devices,) + own.shape, own.dtype),
+        in_specs=[vmem],
+        out_specs=vmem,
+        scratch_shapes=[pltpu.SemaphoreType.DMA((n_devices,)), pltpu.SemaphoreType.DMA((n_devices,))],
+        compiler_params=pltpu.CompilerParams(collective_id=0, has_side_effects=True),
+        name="gather_rows",
+    )(own)
+    return out.reshape(n_devices * own.shape[0], own.shape[1])
+
+
 def attend_kernel(
-    n_parts, n_chunks, width_latent, heads, scale, steps_ref, list_ref, *refs
+    n_parts, n_chunks, first, width_latent, heads, scale, steps_ref, list_ref, *refs
 ):
     cache_in = refs[:n_parts]
     q_refs = refs[n_parts : n_parts + n_chunks]
@@ -57,7 +96,7 @@
     ]
     for copy in copies:
         copy.start()
-    groups, rows_chunk, _ = q_refs[0].shape
+    groups, rows_chunk, _ = o_refs[0].shape
     rows = rows_chunk * n_chunks
     tokens = rows_chunk // heads
     span = STEP * BLK
@@ -71,76 +110,100 @@
         copy.wait()
     base = 2**tokens
 
-    def group(g, carry):
-        query = jnp.concatenate([q[g] for q in q_refs], axis=0)
+    def one_step(i, g, query, s, peak, total):
+        entries = [list_ref[g, s * STEP + k] for k in range(STEP)]
+        key_rows = jnp.concatenate([keys[e // base] for e in entries], axis=0)
+        bits = jnp.zeros((1, span), jnp.int32)
+        for k in range(STEP):
+            bits = jnp.where(block_of_col == k, entries[k] % base, bits)
+        live = (bits & row_bit) != 0
+        scores = (
+            lax.dot_general(
+                query, key_rows, (((1,), (1,)), ((), ())), preferred_element_type=jnp.float32
+            )
+            * scale
+        )
+        scores = jnp.where(live, scores, EMPTY)
+        new_peak = jnp.maximum(peak, jnp.max(scores, axis=1, keepdims=True))
+        fade = jnp.exp(peak - new_peak)
+        exponent = jnp.where(live, jnp.exp(scores - new_peak), 0.0)
+        acc[i] = acc[i] * fade + jnp.dot(
+            exponent.astype(jnp.bfloat16),
+            key_rows[:, :width_latent],
+            preferred_element_type=jnp.float32,
+        )
+        return new_peak, total * fade + jnp.sum(exponent, axis=1, keepdims=True)
+
+    def some_groups(block, carry):
+        local_g = [block * SIDE + i for i in range(SIDE)]
+        g = [first + x for x in local_g]
+        query = [jnp.concatenate([q[x] for q in q_refs], axis=0) for x in g]
         acc[...] = jnp.zeros_like(acc)
 
-        def step(s, state):
-            peak, total = state
-            entries = [list_ref[g, s * STEP + k] for k in range(STEP)]
-            key_rows = jnp.concatenate([keys[e // base] for e in entries], axis=0)
-            bits = jnp.zeros((1, span), jnp.int32)
-            for k in range(STEP):
-                bits = jnp.where(block_of_col == k, entries[k] % base, bits)
-            live = (bits & row_bit) != 0
-            scores = (
-                lax.dot_general(
-                    query, key_rows, (((1,), (1,)), ((), ())), preferred_element_type=jnp.float32
-                )
-                * scale
+        def step(s, states):
+            return tuple(
+                one_step(i, g[i], query[i], s, *states[i]) for i in range(SIDE)
             )
-            scores = jnp.where(live, scores, EMPTY)
-            new_peak = jnp.maximum(peak, jnp.max(scores, axis=1, keepdims=True))
-            fade = jnp.exp(peak - new_peak)
-            exponent = jnp.where(live, jnp.exp(scores - new_peak), 0.0)
-            acc[...] = acc[...] * fade + jnp.dot(
-                exponent.astype(jnp.bfloat16),
-                key_rows[:, :width_latent],
-                preferred_element_type=jnp.float32,
+
+        start = (jnp.full((rows, 1), EMPTY, jnp.float32), jnp.zeros((rows, 1), jnp.float32))
+        n_steps = functools.reduce(jnp.maximum, [steps_ref[x] for x in g])
+        states = lax.fori_loop(0, n_steps, step, (start,) * SIDE)
+        for i in range(SIDE):
+            peak, total = states[i]
+            some = total > 0.0
+            safe = jnp.where(some, total, 1.0)
+            out = (acc[i] / safe).astype(jnp.bfloat16)
+            for j in range(n_chunks):
+                o_refs[j][local_g[i]] = out[j * rows_chunk : (j + 1) * rows_chunk]
+            lse = jnp.where(some, peak + jnp.log(safe), EMPTY)
+            lse_ref[pl.ds(local_g[i], 1), :] = jnp.sum(
+                jnp.where(diagonal, lse, 0.0), axis=0, keepdims=True
             )
-            return new_peak, total * fade + jnp.sum(exponent, axis=1, keepdims=True)
-
-        peak, total = lax.fori_loop(
-            0,
-            steps_ref[g],
-            step,
-            (jnp.full((rows, 1), EMPTY, jnp.float32), jnp.zeros((rows, 1), jnp.float32)),
-        )
-        some = total > 0.0
-        safe = jnp.where(some, total, 1.0)
-        out = (acc[...] / safe).astype(jnp.bfloat16)
-        for j in range(n_chunks):
-            o_refs[j][g] = out[j * rows_chunk : (j + 1) * rows_chunk]
-        lse = jnp.where(some, peak + jnp.log(safe), EMPTY)
-        lse_ref[pl.ds(g, 1), :] = jnp.sum(
-            jnp.where(diagonal, lse, 0.0), axis=0, keepdims=True
-        )
         return carry
 
-    lax.fori_loop(0, groups, group, 0)
-
-
-def attend(parts, chunks, block_list, steps, heads, width_latent, scale):
+    lax.fori_loop(0, groups // SIDE, some_groups, 0)
+
+
+def attend(parts, chunks, block_list, steps, first, groups, heads, width_latent, scale):
     n_parts, n_chunks = len(parts), len(chunks)
     part_blocks, _, width_row = parts[0].shape
-    groups, rows_chunk, _ = chunks[0].shape
+    rows_chunk = chunks[0].shape[1]
     vmem = pl.BlockSpec(memory_space=pltpu.VMEM)
     smem = pl.BlockSpec(memory_space=pltpu.SMEM)
     out = pl.pallas_call(
-        functools.partial(attend_kernel, n_parts, n_chunks, width_latent, heads, scale),
+        functools.partial(attend_kernel, n_parts, n_chunks, first, width_latent, heads, scale),
         out_shape=[jax.ShapeDtypeStruct((groups, rows_chunk, width_latent), jnp.bfloat16)] * n_chunks
         + [jax.ShapeDtypeStruct((groups, rows_chunk * n_chunks), jnp.float32)],
         in_specs=[smem, smem] + [pl.BlockSpec(memory_space=pl.ANY)] * n_parts + [vmem] * n_chunks,
         out_specs=[vmem] * (n_chunks + 1),
         scratch_shapes=[
             pltpu.VMEM((n_parts * part_blocks, BLK, width_row), jnp.bfloat16),
-            pltpu.VMEM((rows_chunk * n_chunks, width_latent), jnp.float32),
+            pltpu.VMEM((SIDE, rows_chunk * n_chunks, width_latent), jnp.float32),
             pltpu.SemaphoreType.DMA((n_parts,)),
         ],
         compiler_params=pltpu.CompilerParams(vmem_limit_bytes=48 * 2**20),
         name="attend",
+        cost_estimate=pl.CostEstimate(
+            flops=2 * groups * rows_chunk * n_chunks * part_blocks * BLK * (width_row + width_latent),
+            bytes_accessed=2 * n_parts * part_blocks * BLK * width_row,
+            transcendentals=0,
+        ),
     )(steps, block_list, *parts, *chunks)
     return out[:n_chunks], out[n_chunks]
+
+
+def combine(partials):
+    if len(partials) == 1:
+        return partials[0]
+    logs = [log for _, log in partials]
+    top = functools.reduce(jnp.maximum, logs)
+    shares = [jnp.exp(x - top) for x in logs]
+    total = functools.reduce(jnp.add, shares)
+    value = functools.reduce(
+        jnp.add,
+        [v.astype(jnp.float32) * (s / total)[:, :, None] for (v, _), s in zip(partials, shares)],
+    ).astype(jnp.bfloat16)
+    return value, top + jnp.log(total)
 
 
 def local(
@@ -166,13 +229,6 @@
         jnp.concatenate([scaled_t.reshape(width_latent, -1), cache_t[width_latent:]], axis=0)
         .T.reshape(blocks_local, BLK, width_row)
     )
-    parts = [own_cache]
-    for bit in reversed(cache_bits):
-        parts = parts + [xor_permute(p, n_devices, bit) for p in parts]
-    parts_masks = [0]
-    for bit in reversed(cache_bits):
-        parts_masks = parts_masks + [m | bit for m in parts_masks]
-
     latent_f = q_latent.astype(jnp.float32)
     normed = (
         latent_f
@@ -181,15 +237,30 @@
     ).astype(jnp.bfloat16)
     live_sel = jnp.arange(top_blocks, dtype=jnp.int32)[None, :] < counts[:, None]
     owner = jnp.where(live_sel, selected // blocks_local, -1)
+    row_width = normed.shape[1] + 2 * top_blocks
     packed = jnp.concatenate(
-        [normed, owner.astype(jnp.bfloat16), (selected % blocks_local).astype(jnp.bfloat16)], axis=1
-    )
-    gathered = lax.all_gather(packed, "ctx", axis=0, tiled=True)
+        [
+            normed,
+            owner.astype(jnp.bfloat16),
+            (selected % blocks_local).astype(jnp.bfloat16),
+            jnp.zeros((q_local, -row_width % 128), jnp.bfloat16),
+        ],
+        axis=1,
+    )
+    gathered = gather_rows(packed, n_devices)
+    gathered, own_cache = lax.optimization_barrier((gathered, own_cache))
+    parts = [own_cache]
+    for bit in reversed(cache_bits):
+        parts = parts + [xor_permute(p, n_devices, bit) for p in parts]
+    parts_masks = [0]
+    for bit in reversed(cache_bits):
+        parts_masks = parts_masks + [m | bit for m in parts_masks]
+
     row_count = gathered.shape[0]
     latent_width = normed.shape[1]
     all_normed = gathered[:, :latent_width]
     all_owner = gathered[:, latent_width : latent_width + top_blocks].astype(jnp.int32)
-    all_inner = gathered[:, latent_width + top_blocks :].astype(jnp.int32)
+    all_inner = gathered[:, latent_width + top_blocks : row_width].astype(jnp.int32)
 
     projected = jnp.dot(all_normed, w_uq, preferred_element_type=jnp.float32).reshape(
         row_count, heads_local, width_content + width_rotary
@@ -229,20 +300,26 @@
     steps = (jnp.sum(needed, axis=1) + STEP - 1) // STEP
 
     scale = 1.0 / math.sqrt(width_content + width_rotary)
-    outs, lse = attend(parts, chunks, block_list, steps, heads_local, width_latent, scale)
-
     rows_chunk = q_local * heads_local
-    values, logs = [], []
-    for i, mask in enumerate(chunk_masks):
-        part_lse = lse[:, i * rows_chunk : (i + 1) * rows_chunk]
-        values.append(outs[i] if mask == 0 else xor_permute(outs[i], n_devices, mask))
-        logs.append(part_lse if mask == 0 else xor_permute(part_lse, n_devices, mask))
-    top = functools.reduce(jnp.maximum, logs)
-    shares = [jnp.exp(x - top) for x in logs]
-    total = functools.reduce(jnp.add, shares)
-    latent_out = functools.reduce(
-        jnp.add, [v.astype(jnp.float32) * (s / total)[:, :, None] for v, s in zip(values, shares)]
-    ).astype(jnp.bfloat16)
+    groups_call = groups // SPLIT
+    halves = []
+    for first in range(0, groups, groups_call):
+        outs, lse = attend(
+            parts, chunks, block_list, steps, first, groups_call, heads_local, width_latent, scale
+        )
+        held_for = {
+            mask: [(outs[i], lse[:, i * rows_chunk : (i + 1) * rows_chunk])]
+            for i, mask in enumerate(chunk_masks)
+        }
+        for bit in query_bits:
+            leaving = sorted([m for m in held_for if m & bit], reverse=True)
+            going = [combine(held_for.pop(m)) for m in leaving]
+            logs = xor_permute(jnp.stack([log for _, log in going]), n_devices, bit)
+            for i, mask in enumerate(leaving):
+                value = xor_permute(going[i][0], n_devices, bit)
+                held_for[mask ^ bit].append((value, logs[i]))
+        halves.append(combine(held_for[0])[0])
+    latent_out = jnp.concatenate(halves, axis=0)
     head_out = latent_out.reshape(row_count, heads_local, width_latent)
     head_values = jnp.einsum(
         "qhc,hcv->qhv", head_out, w_uv, preferred_element_type=jnp.float32

time: 272 us -> 237 us (0.87); the launches traced: 267 us -> 237 us
  blocking collectives: 72.6 us -> 0 us
  waiting for transfers between devices: 111 us -> 151 us
  starting transfers between devices: 9.95 us -> 17.8 us
  Pallas kernels: 43.5 us -> 38 us
    all_gather x1 -> x0, blocking collectives: 72.6 us -> none  [local(): gathered = lax.all_gather(packed, 'ctx', axis=0, tiled=True)]
    ppermute x16 -> x15, waiting for transfers between devices: 111 us -> 151 us  [xor_permute(): lax.ppermute(value, 'ctx', [(i, i ^ distance) for i in range(n_devices)])]
    ppermute x16 -> x15, starting transfers between devices: 9.95 us -> 17.8 us  [xor_permute(): lax.ppermute(value, 'ctx', [(i, i ^ distance) for i in range(n_devices)])]
    pallas_call x1 -> x2, Pallas kernels: 43.5 us -> 38 us  [the longest x1 26.3 us: attend(): pl.pallas_call(functools.partial(attend_kernel, n_parts, n_chunks, first,...]
  transfers between devices with their start and end apart: 16 -> 15, of which waited for: 8 -> 11; matrix products, arithmetic and copies ran while one was open for 3% -> 3% of each run, Pallas kernels for 0% -> 0%
where the time goes in v2:
time: 237 us
  waiting for transfers between devices  151 us (64%)
  Pallas kernels  38 us (16%)
  starting transfers between devices  17.8 us (8%)
  matrix products  12.2 us (5%)
  other arithmetic  10.1 us (4%)
  local copies, waits for them, and re-layouts  8.26 us (3%)
    ppermute x15, waiting for transfers between devices, xor_permute(): lax.ppermute(value, 'ctx', [(i, i ^ distance) for i in range(n_devices)])  151 us
    pallas_call x1, Pallas kernels, attend(): pl.pallas_call(functools.partial(attend_kernel, n_parts, n_chunks, first,...  26.3 us
    ppermute x15, starting transfers between devices, xor_permute(): lax.ppermute(value, 'ctx', [(i, i ^ distance) for i in range(n_devices)])  17.8 us
    pallas_call x1, Pallas kernels, gather_rows(): pl.pallas_call(functools.partial(gather_kernel, n_devices), out_shape=jax...  11.7 us
    dot_general x1, matrix products, local(): result = jnp.dot(head_values, w_o, preferred_element_type=jnp.float32)  8.28 us
  transfers between devices with their start and end apart: 15, of which 11 were waited for; matrix products, arithmetic and copies ran while one was open for 3% of the time, Pallas kernels for 0%

profile of v2, /device:TPU:0, one launch (start us, length us, event | category | flops | bytes accessed | tf_op | source)
XLA Modules:
  0.0 237.2 jit_solution(7318568809224294968)
XLA Ops:
  0.0 1.1 slice.61
  1.1 2.2 fusion.2
  3.2 0.2 maximum_bitcast_fusion
  3.5 2.6 %copy.24 = bf16[2048,576]{1,0:T(8,128)(2,1)} copy(bf16[2048,576]{0,1:T(8,128)(2,1)S(1)} %maximum_bitcast_fusion) | data formatting | bytes 4718592 | tf_op jit(solution)/shard_map/transpose | solution.py:230
  6.0 0.1 fusion.18
  6.4 0.7 concatenate.12.own_ref
  7.1 11.7 %gather_rows.1 = bf16[16,4,1664]{2,1,0:T(4,128)(2,1)} custom-call(bf16[4,1664]{1,0:T(4,128)(2,1)} %concatenate.12.own_ref), custom_call_target="tpu_custom_call" | custom-call | tf_op jit(solution)/shard_map/gather_rows/pallas_call | solution.py:71
  18.8 1.0 reshape.141
  19.8 2.3 collective-permute-start
  22.0 3.3 %fusion.10 = f32[64,1536]{1,0:T(8,128)S(1)} fusion(bf16[1536,1536]{1,0:T(8,128)(2,1)} %param.12, bf16[64,1664]{1,0:T(8,128)(2,1)S(1)} %reshape.141), kind=kOutput, calls=%fused_computation.29 | convolution fusion | flops 301989888 | bytes 5308416 | tf_op jit(solution)/shard_map/dot_general | solution.py:265
  25.3 0.2 reshape.143
  25.5 0.2 multiply_cosine_fusion
  25.7 0.1 fusion.30
  25.9 53.6 %collective-permute-done.refs_1_ = bf16[32,64,576]{2,1,0:T(8,128)(2,1)} collective-permute-done((bf16[32,64,576]{2,1,0:T(8,128)(2,1)}, bf16[32,64,576]{2,1,0:T(8,128)(2,1)}, u32[]{:S(2)}, u32[]{:S(2)}) %collective-permute-start) | collective-permute-done | bytes 2359328 | tf_op jit(solution)/shard_map/ppermute | solution.py:36
  79.6 0.3 fusion.3
  79.9 0.1 pad_maximum_fusion
  80.0 0.4 copy.29
  80.4 1.9 collective-permute-start.3
  82.3 2.2 collective-permute-start.4
  84.5 0.9 fusion.15
  85.4 0.4 fusion.5
  85.9 0.3 reduce_window_sum.11
  86.2 0.1 convert_subtract_fusion
  86.3 26.3 %collective-permute-done.3.refs_5_ = bf16[16,32,576]{2,1,0:T(8,128)(2,1)S(1)} collective-permute-done((bf16[16,32,576]{2,1,0:T(8,128)(2,1)S(1)}, bf16[16,32,576]{2,1,0:T(8,128)(2,1)S(1)}, u32[]{:S(2)}, u32[]{:S(2)}) %collective-permute-start.3) | collective-permute-done | bytes 589856 | tf_op jit(solution)/shard_map/ppermute | solution.py:36
  112.6 1.2 select_reduce_fusion.list_ref
  113.8 15.1 %collective-permute-done.5.refs_7_ = bf16[16,32,576]{2,1,0:T(8,128)(2,1)S(1)} collective-permute-done((bf16[16,32,576]{2,1,0:T(8,128)(2,1)S(1)}, bf16[16,32,576]{2,1,0:T(8,128)(2,1)S(1)}, u32[]{:S(2)}, u32[]{:S(2)}) %collective-permute-start.5) | collective-permute-done | bytes 589856 | tf_op jit(solution)/shard_map/ppermute | solution.py:36
  128.9 26.3 %attend.1 = (bf16[16,32,512]{2,1,0:T(8,128)(2,1)S(1)}, bf16[16,32,512]{2,1,0:T(8,128)(2,1)S(1)}, bf16[16,32,512]{2,1,0:T(8,128)(2,1)}, bf16[16,32,512]{2,1,0:T(8,128)(2,1)S(1)}, f32[16,128]{1,0:T(8,128)S(1)}) custom-call(s32[16]{0:T(128)S(1)} %and_select_fusion.steps_ref, s32[16,128]{1,0:T(8,128)S(1)} %select_reduce_fusion.list_ref, ...), custom_call_target="tpu_custom_call" | custom-call | flops 9126805504 | bytes 9437184 | tf_op jit(solution)/shard_map/attend/pallas_call | solution.py:173
  155.3 7.2 %collective-permute-start.9 = (bf16[16,32,512]{2,1,0:T(8,128)(2,1)S(1)}, bf16[16,32,512]{2,1,0:T(8,128)(2,1)S(1)}, u32[]{:S(2)}, u32[]{:S(2)}) collective-permute-start(bf16[16,32,512]{2,1,0:T(8,128)(2,1)S(1)} %get-tuple-element.18), channel_id=1, source_target_pairs={{0,4},{1,5},{2,6},{3,7},{4,0},{5,1},{6,2},{7,3},{8,12},{9,13},{10,... | collective-permute-start | bytes 1572872 | tf_op jit(solution)/shard_map/ppermute | solution.py:36
  162.5 11.5 %collective-permute-done.6 = f32[2,16,32]{2,1,0:T(8,128)S(1)} collective-permute-done((f32[2,16,32]{2,1,0:T(8,128)S(1)}, f32[2,16,32]{2,1,0:T(8,128)S(1)}, u32[]{:S(2)}, u32[]{:S(2)}) %collective-permute-start.6) | collective-permute-done | bytes 4128 | tf_op jit(solution)/shard_map/ppermute | solution.py:36
  174.2 1.9 collective-permute-start.8
  176.1 2.7 %collective-permute-done.7 = f32[1,16,32]{2,1,0:T(8,128)S(1)} collective-permute-done((f32[1,16,32]{2,1,0:T(8,128)S(1)}, f32[1,16,32]{2,1,0:T(8,128)S(1)}, u32[]{:S(2)}, u32[]{:S(2)}) %collective-permute-start.7) | collective-permute-done | bytes 2080 | tf_op jit(solution)/shard_map/ppermute | solution.py:36
  178.9 0.3 add_convert_fusion.1
  179.3 0.2 collective-permute-start.10
  179.4 16.6 %collective-permute-done.8 = bf16[16,32,512]{2,1,0:T(8,128)(2,1)} collective-permute-done((bf16[16,32,512]{2,1,0:T(8,128)(2,1)}, bf16[16,32,512]{2,1,0:T(8,128)(2,1)}, u32[]{:S(2)}, u32[]{:S(2)}) %collective-permute-start.8) | collective-permute-done | bytes 524320 | tf_op jit(solution)/shard_map/ppermute | solution.py:36
  196.0 6.9 %collective-permute-done.10 = bf16[16,32,512]{2,1,0:T(8,128)(2,1)} collective-permute-done((bf16[16,32,512]{2,1,0:T(8,128)(2,1)S(1)}, bf16[16,32,512]{2,1,0:T(8,128)(2,1)}, u32[]{:S(2)}, u32[]{:S(2)}) %collective-permute-start.10) | collective-permute-done | bytes 524320 | tf_op jit(solution)/shard_map/ppermute | solution.py:36
  202.9 1.6 add_convert_fusion
  204.5 0.4 fusion.4
  205.0 8.3 %fusion = f32[2,2,2,2,4,7168]{5,4,3,2,1,0:T(4,128)S(1)} fusion(bf16[2,2,2,2,4,1024]{5,4,3,2,1,0:T(4,128)(2,1)S(1)} %dot_general.17, bf16[1024,7168]{1,0:T(8,128)(2,1)} %param.15), kind=kOutput, calls=%fused_computation | convolution fusion | flops 939524096 | bytes 16646144 | tf_op jit(solution)/shard_map/dot_general | solution.py:328
  213.3 0.9 fusion.8
  214.2 2.0 collective-permute-done.11
  216.2 0.2 bitcast_add_fusion
  216.5 0.9 copy-done.1
  217.5 1.8 collective-permute-start.12
  219.3 5.9 %collective-permute-done.12 = bf16[2,2,4,7168]{3,2,1,0:T(4,128)(2,1)S(1)} collective-permute-done((bf16[2,2,4,7168]{3,2,1,0:T(4,128)(2,1)S(1)}, bf16[2,2,4,7168]{3,2,1,0:T(4,128)(2,1)S(1)}, u32[]{:S(2)}, u32[]{:S(2)}) %collective-permute-start.12) | collective-permute-done | bytes 229408 | tf_op jit(solution)/shard_map/ppermute | solution.py:36
  225.2 1.1 bitcast_add_fusion.1
  226.5 4.7 %collective-permute-done.13 = bf16[2,4,7168]{2,1,0:T(4,128)(2,1)S(1)} collective-permute-done((bf16[2,4,7168]{2,1,0:T(4,128)(2,1)S(1)}, bf16[2,4,7168]{2,1,0:T(4,128)(2,1)S(1)}, u32[]{:S(2)}, u32[]{:S(2)}) %collective-permute-start.13) | collective-permute-done | bytes 114720 | tf_op jit(solution)/shard_map/ppermute | solution.py:36
  231.5 5.1 %collective-permute-done.14 = bf16[4,7168]{1,0:T(4,128)(2,1)S(1)} collective-permute-done((bf16[4,7168]{1,0:T(4,128)(2,1)S(1)}, bf16[4,7168]{1,0:T(4,128)(2,1)S(1)}, u32[]{:S(2)}, u32[]{:S(2)}) %collective-permute-start.14) | collective-permute-done | bytes 57376 | tf_op jit(solution)/shard_map/ppermute | solution.py:36
  236.6 0.7 fusion.13
  (52 shorter events, 1.4 us)
Async XLA Ops:
  0.0 79.6 %copy-start = (bf16[8,128,512]{2,1,0:T(8,128)(2,1)S(1)}, bf16[8,128,512]{2,1,0:T(8,128)(2,1)}, u32[]{:S(2)}) copy-start(bf16[8,128,512]{2,1,0:T(8,128)(2,1)} %param.13) | copy-start | bytes 3145732
  3.4 2.6 %copy-start.4 = (bf16[4,1536]{1,0:T(4,128)(2,1)S(1)}, bf16[4,1536]{1,0:T(4,128)(2,1)}, u32[]{:S(2)}) copy-start(bf16[4,1536]{1,0:T(4,128)(2,1)} %param.10) | copy-start | bytes 36868
  3.4 2.8 %copy-start.6 = (s32[4,32]{1,0:T(4,128)S(1)}, s32[4,32]{1,0:T(4,128)}, u32[]{:S(2)}) copy-start(s32[4,32]{1,0:T(4,128)} %param.18) | copy-start | bytes 1540
  3.4 2.8 %copy-start.7 = (s32[4]{0:T(128)S(1)}, s32[4]{0:T(128)}, u32[]{:S(2)}) copy-start(s32[4]{0:T(128)} %param.19) | copy-start | bytes 52
  3.5 2.8 %copy-start.5 = (f32[1536]{0:T(1024)S(1)}, f32[1536]{0:T(1024)}, u32[]{:S(2)}) copy-start(f32[1536]{0:T(1024)} %param.11) | copy-start | bytes 18436
  19.7 2.3 copy-start.3
  19.8 59.7 %collective-permute-start = (bf16[32,64,576]{2,1,0:T(8,128)(2,1)}, bf16[32,64,576]{2,1,0:T(8,128)(2,1)}, u32[]{:S(2)}, u32[]{:S(2)}) collective-permute-start(bf16[32,64,576]{2,1,0:T(8,128)(2,1)} %bitcast.113), channel_id=1, source_target_pairs={{0,2},{1,3},{2,0},{3,1},{4,6},{5,7},{6,4},{7,5},{8,10},{9,11},{10,... | collective-permute-start | bytes 7077896 | tf_op jit(solution)/shard_map/ppermute | solution.py:36
  22.0 106.8 %collective-permute-start.1 = (bf16[32,64,576]{2,1,0:T(8,128)(2,1)}, bf16[32,64,576]{2,1,0:T(8,128)(2,1)}, u32[]{:S(2)}, u32[]{:S(2)}) collective-permute-start(bf16[32,64,576]{2,1,0:T(8,128)(2,1)} %bitcast.114), channel_id=1, source_target_pairs={{0,1},{1,0},{2,3},{3,2},{4,5},{5,4},{6,7},{7,6},{8,9},{9,8},{10,11... | collective-permute-start | bytes 7077896 | tf_op jit(solution)/shard_map/ppermute | solution.py:36
  79.5 49.4 %collective-permute-start.2 = (bf16[32,64,576]{2,1,0:T(8,128)(2,1)}, bf16[32,64,576]{2,1,0:T(8,128)(2,1)}, u32[]{:S(2)}, u32[]{:S(2)}) collective-permute-start(bf16[32,64,576]{2,1,0:T(8,128)(2,1)} %collective-permute-done.refs_1_), channel_id=1, source_target_pairs={{0,1},{1,0},{2,3},{3,2},{4,5},{5,4},{6,7},{7,6},{8,9},{9,8},{10,11... | collective-permute-start | bytes 7077896 | tf_op jit(solution)/shard_map/ppermute | solution.py:36
  80.4 32.2 %collective-permute-start.3 = (bf16[16,32,576]{2,1,0:T(8,128)(2,1)S(1)}, bf16[16,32,576]{2,1,0:T(8,128)(2,1)S(1)}, u32[]{:S(2)}, u32[]{:S(2)}) collective-permute-start(bf16[16,32,576]{2,1,0:T(8,128)(2,1)S(1)} %bitcast.110), channel_id=1, source_target_pairs={{0,8},{1,9},{2,10},{3,11},{4,12},{5,13},{6,14},{7,15},{8,0},{9,1},... | collective-permute-start | bytes 1769480 | tf_op jit(solution)/shard_map/ppermute | solution.py:36
  82.3 31.5 %collective-permute-start.4 = (bf16[16,32,576]{2,1,0:T(8,128)(2,1)S(1)}, bf16[16,32,576]{2,1,0:T(8,128)(2,1)S(1)}, u32[]{:S(2)}, u32[]{:S(2)}) collective-permute-start(bf16[16,32,576]{2,1,0:T(8,128)(2,1)S(1)} %bitcast.111), channel_id=1, source_target_pairs={{0,4},{1,5},{2,6},{3,7},{4,0},{5,1},{6,2},{7,3},{8,12},{9,13},{10,... | collective-permute-start | bytes 1769480 | tf_op jit(solution)/shard_map/ppermute | solution.py:36
  112.6 16.3 %collective-permute-start.5 = (bf16[16,32,576]{2,1,0:T(8,128)(2,1)S(1)}, bf16[16,32,576]{2,1,0:T(8,128)(2,1)S(1)}, u32[]{:S(2)}, u32[]{:S(2)}) collective-permute-start(bf16[16,32,576]{2,1,0:T(8,128)(2,1)S(1)} %collective-permute-done.3.refs_5_), channel_id=1, source_target_pairs={{0,4},{1,5},{2,6},{3,7},{4,0},{5,1},{6,2},{7,3},{8,12},{9,13},{10,... | collective-permute-start | bytes 1769480 | tf_op jit(solution)/shard_map/ppermute | solution.py:36
  155.2 49.3 %copy-start.2 = (bf16[8,512,128]{2,1,0:T(8,128)(2,1)S(1)}, bf16[8,512,128]{2,1,0:T(8,128)(2,1)}, u32[]{:S(2)}) copy-start(bf16[8,512,128]{2,1,0:T(8,128)(2,1)} %param.14) | copy-start | bytes 3145732
  155.3 23.7 %collective-permute-start.9 = (bf16[16,32,512]{2,1,0:T(8,128)(2,1)S(1)}, bf16[16,32,512]{2,1,0:T(8,128)(2,1)S(1)}, u32[]{:S(2)}, u32[]{:S(2)}) collective-permute-start(bf16[16,32,512]{2,1,0:T(8,128)(2,1)S(1)} %get-tuple-element.18), channel_id=1, source_target_pairs={{0,4},{1,5},{2,6},{3,7},{4,0},{5,1},{6,2},{7,3},{8,12},{9,13},{10,... | collective-permute-start | bytes 1572872 | tf_op jit(solution)/shard_map/ppermute | solution.py:36
  162.5 11.6 %collective-permute-start.6 = (f32[2,16,32]{2,1,0:T(8,128)S(1)}, f32[2,16,32]{2,1,0:T(8,128)S(1)}, u32[]{:S(2)}, u32[]{:S(2)}) collective-permute-start(f32[2,16,32]{2,1,0:T(8,128)S(1)} %pad_maximum_fusion.1), channel_id=1, source_target_pairs={{0,4},{1,5},{2,6},{3,7},{4,0},{5,1},{6,2},{7,3},{8,12},{9,13},{10,... | collective-permute-start | bytes 12296 | tf_op jit(solution)/shard_map/ppermute | solution.py:36
  174.1 4.7 %collective-permute-start.7 = (f32[1,16,32]{2,1,0:T(8,128)S(1)}, f32[1,16,32]{2,1,0:T(8,128)S(1)}, u32[]{:S(2)}, u32[]{:S(2)}) collective-permute-start(f32[1,16,32]{2,1,0:T(8,128)S(1)} %add_bitcast_fusion), channel_id=1, source_target_pairs={{0,8},{1,9},{2,10},{3,11},{4,12},{5,13},{6,14},{7,15},{8,0},{9,1},... | collective-permute-start | bytes 6152 | tf_op jit(solution)/shard_map/ppermute | solution.py:36
  174.2 21.8 %collective-permute-start.8 = (bf16[16,32,512]{2,1,0:T(8,128)(2,1)}, bf16[16,32,512]{2,1,0:T(8,128)(2,1)}, u32[]{:S(2)}, u32[]{:S(2)}) collective-permute-start(bf16[16,32,512]{2,1,0:T(8,128)(2,1)} %get-tuple-element.16), channel_id=1, source_target_pairs={{0,4},{1,5},{2,6},{3,7},{4,0},{5,1},{6,2},{7,3},{8,12},{9,13},{10,... | collective-permute-start | bytes 1572872 | tf_op jit(solution)/shard_map/ppermute | solution.py:36
  179.3 23.6 %collective-permute-start.10 = (bf16[16,32,512]{2,1,0:T(8,128)(2,1)S(1)}, bf16[16,32,512]{2,1,0:T(8,128)(2,1)}, u32[]{:S(2)}, u32[]{:S(2)}) collective-permute-start(bf16[16,32,512]{2,1,0:T(8,128)(2,1)S(1)} %add_convert_fusion.1), channel_id=1, source_target_pairs={{0,8},{1,9},{2,10},{3,11},{4,12},{5,13},{6,14},{7,15},{8,0},{9,1},... | collective-permute-start | bytes 1572872 | tf_op jit(solution)/shard_map/ppermute | solution.py:36
  214.2 2.0 collective-permute-start.11
  216.5 0.9 copy-start.1
  217.5 7.7 %collective-permute-start.12 = (bf16[2,2,4,7168]{3,2,1,0:T(4,128)(2,1)S(1)}, bf16[2,2,4,7168]{3,2,1,0:T(4,128)(2,1)S(1)}, u32[]{:S(2)}, u32[]{:S(2)}) collective-permute-start(bf16[2,2,4,7168]{3,2,1,0:T(4,128)(2,1)S(1)} %fusion.9), channel_id=1, source_target_pairs={{0,2},{1,3},{2,0},{3,1},{4,6},{5,7},{6,4},{7,5},{8,10},{9,11},{10,... | collective-permute-start | bytes 688136 | tf_op jit(solution)/shard_map/ppermute | solution.py:36
  226.4 4.9 %collective-permute-start.13 = (bf16[2,4,7168]{2,1,0:T(4,128)(2,1)S(1)}, bf16[2,4,7168]{2,1,0:T(4,128)(2,1)S(1)}, u32[]{:S(2)}, u32[]{:S(2)}) collective-permute-start(bf16[2,4,7168]{2,1,0:T(4,128)(2,1)S(1)} %fusion.12), channel_id=1, source_target_pairs={{0,4},{1,5},{2,6},{3,7},{4,0},{5,1},{6,2},{7,3},{8,12},{9,13},{10,... | collective-permute-start | bytes 344072 | tf_op jit(solution)/shard_map/ppermute | solution.py:36
  231.4 5.2 %collective-permute-start.14 = (bf16[4,7168]{1,0:T(4,128)(2,1)S(1)}, bf16[4,7168]{1,0:T(4,128)(2,1)S(1)}, u32[]{:S(2)}, u32[]{:S(2)}) collective-permute-start(bf16[4,7168]{1,0:T(4,128)(2,1)S(1)} %fusion.14), channel_id=1, source_target_pairs={{0,8},{1,9},{2,10},{3,11},{4,12},{5,13},{6,14},{7,15},{8,0},{9,1},... | collective-permute-start | bytes 172040 | tf_op jit(solution)/shard_map/ppermute | solution.py:36

commit v3 on v2

--- a/solution.py
+++ b/solution.py
@@ -34,13 +34,6 @@
 
 def xor_permute(value, n_devices, distance):
     return lax.ppermute(value, "ctx", [(i, i ^ distance) for i in range(n_devices)])
-
-
-def masks_of(bits):
-    out = [0]
-    for bit in bits:
-        out += [o | bit for o in out]
-    return out
 
 
 def gather_kernel(n_devices, own_ref, out_ref, send_sems, recv_sems):
@@ -217,8 +210,7 @@
     q_local, top_blocks = selected.shape
     blocks_local = latent_cache.shape[0] // BLK
     tiles = kv_scales.shape[1]
-    cache_masks, query_masks = masks_of(cache_bits), masks_of(query_bits)
-    n_parts = len(cache_masks)
+    n_parts = 2 ** len(cache_bits)
 
     cache_t = latent_cache.T
     scaled_t = (
@@ -249,13 +241,10 @@
     )
     gathered = gather_rows(packed, n_devices)
     gathered, own_cache = lax.optimization_barrier((gathered, own_cache))
-    parts = [own_cache]
-    for bit in reversed(cache_bits):
-        parts = parts + [xor_permute(p, n_devices, bit) for p in parts]
-    parts_masks = [0]
-    for bit in reversed(cache_bits):
-        parts_masks = parts_masks + [m | bit for m in parts_masks]
-
+    near_bit, far_bit = cache_bits
+    far = xor_permute(own_cache, n_devices, far_bit)
+    near = xor_permute(own_cache, n_devices, near_bit)
+    parts_masks = [0, far_bit, near_bit, far_bit | near_bit]
     row_count = gathered.shape[0]
     latent_width = normed.shape[1]
     all_normed = gathered[:, :latent_width]
@@ -280,6 +269,9 @@
     for bit in reversed(query_bits):
         chunks = chunks + [xor_permute(c, n_devices, bit) for c in chunks]
         chunk_masks = chunk_masks + [m | bit for m in chunk_masks]
+
+    far, chunks[-1] = lax.optimization_barrier((far, chunks[-1]))
+    parts = [own_cache, far, near, xor_permute(far, n_devices, near_bit)]
 
     n_held = n_parts * blocks_local
     place = jnp.full_like(all_owner, -1)

time: 237 us -> 209 us (0.88)
  waiting for transfers between devices: 151 us -> 115 us
  starting transfers between devices: 17.8 us -> 28.2 us
    ppermute x15, waiting for transfers between devices: 151 us -> 115 us  [xor_permute(): lax.ppermute(value, 'ctx', [(i, i ^ distance) for i in range(n_devices)])]
    ppermute x15, starting transfers between devices: 17.8 us -> 28.2 us  [xor_permute(): lax.ppermute(value, 'ctx', [(i, i ^ distance) for i in range(n_devices)])]
  transfers between devices with their start and end apart: 15 -> 15, of which waited for: 11 -> 12; matrix products, arithmetic and copies ran while one was open for 3% -> 4% of each run, Pallas kernels for 0% -> 0%
where the time goes in v3:
time: 209 us; the launch traced here: 210 us
  waiting for transfers between devices  115 us (55%)
  Pallas kernels  36.1 us (17%)
  starting transfers between devices  28.2 us (13%)
  matrix products  12.2 us (6%)
  other arithmetic  10.1 us (5%)
  local copies, waits for them, and re-layouts  8.26 us (4%)
    ppermute x15, waiting for transfers between devices, xor_permute(): lax.ppermute(value, 'ctx', [(i, i ^ distance) for i in range(n_devices)])  115 us
    ppermute x15, starting transfers between devices, xor_permute(): lax.ppermute(value, 'ctx', [(i, i ^ distance) for i in range(n_devices)])  28.2 us
    pallas_call x1, Pallas kernels, attend(): pl.pallas_call(functools.partial(attend_kernel, n_parts, n_chunks, first,...  24.4 us
    pallas_call x1, Pallas kernels, gather_rows(): pl.pallas_call(functools.partial(gather_kernel, n_devices), out_shape=jax...  11.7 us
    dot_general x1, matrix products, local(): result = jnp.dot(head_values, w_o, preferred_element_type=jnp.float32)  8.28 us
  transfers between devices with their start and end apart: 15, of which 12 were waited for; matrix products, arithmetic and copies ran while one was open for 4% of the time, Pallas kernels for 0%

profile of v3, /device:TPU:0, one launch (start us, length us, event | category | flops | bytes accessed | tf_op | source)
XLA Modules:
  0.0 210.3 jit_solution(4443156661607942264)
XLA Ops:
  0.0 1.1 slice.61
  1.1 2.2 %fusion.2 = bf16[512,2048]{1,0:T(8,128)(2,1)S(1)} fusion(bf16[576,2048]{1,0:T(8,128)(2,1)} %bitcast.114, f32[4,2048]{1,0:T(4,128)} %bitcast.117), kind=kLoop, calls=%fused_computation.3 | loop fusion | flops 3145728 | bytes 4227072 | tf_op jit(solution)/shard_map/convert_element_type | solution.py:219
  3.2 0.2 maximum_bitcast_fusion
  3.5 2.6 %copy.24 = bf16[2048,576]{1,0:T(8,128)(2,1)} copy(bf16[2048,576]{0,1:T(8,128)(2,1)S(1)} %maximum_bitcast_fusion) | data formatting | bytes 4718592 | tf_op jit(solution)/shard_map/transpose | solution.py:222
  6.4 0.7 concatenate.12.own_ref
  7.1 11.7 %gather_rows.1 = bf16[16,4,1664]{2,1,0:T(4,128)(2,1)} custom-call(bf16[4,1664]{1,0:T(4,128)(2,1)} %concatenate.12.own_ref), custom_call_target="tpu_custom_call" | custom-call | tf_op jit(solution)/shard_map/gather_rows/pallas_call | solution.py:64
  18.8 1.0 reshape.141
  19.8 2.3 %collective-permute-start = (bf16[32,64,576]{2,1,0:T(8,128)(2,1)}, bf16[32,64,576]{2,1,0:T(8,128)(2,1)}, u32[]{:S(2)}, u32[]{:S(2)}) collective-permute-start(bf16[32,64,576]{2,1,0:T(8,128)(2,1)} %bitcast.4.refs_0_), channel_id=1, source_target_pairs={{0,2},{1,3},{2,0},{3,1},{4,6},{5,7},{6,4},{7,5},{8,10},{9,11},{10,... | collective-permute-start | bytes 7077896 | tf_op jit(solution)/shard_map/ppermute | solution.py:36
  22.0 3.3 %fusion.10 = f32[64,1536]{1,0:T(8,128)S(1)} fusion(bf16[1536,1536]{1,0:T(8,128)(2,1)} %param.12, bf16[64,1664]{1,0:T(8,128)(2,1)S(1)} %reshape.141), kind=kOutput, calls=%fused_computation.29 | convolution fusion | flops 301989888 | bytes 5308416 | tf_op jit(solution)/shard_map/dot_general | solution.py:254
  25.3 0.2 reshape.143
  25.5 0.2 multiply_cosine_fusion
  25.7 0.1 fusion.30
  26.0 0.3 fusion.3
  26.4 0.4 copy.29
  26.8 1.9 collective-permute-start.1
  28.7 29.6 %collective-permute-done.1.refs_5_ = bf16[16,32,576]{2,1,0:T(8,128)(2,1)S(1)} collective-permute-done((bf16[16,32,576]{2,1,0:T(8,128)(2,1)S(1)}, bf16[16,32,576]{2,1,0:T(8,128)(2,1)S(1)}, u32[]{:S(2)}, u32[]{:S(2)}) %collective-permute-start.1) | collective-permute-done | bytes 589856 | tf_op jit(solution)/shard_map/ppermute | solution.py:36
  58.3 15.6 %collective-permute-done.2.refs_7_ = bf16[16,32,576]{2,1,0:T(8,128)(2,1)S(1)} collective-permute-done((bf16[16,32,576]{2,1,0:T(8,128)(2,1)S(1)}, bf16[16,32,576]{2,1,0:T(8,128)(2,1)S(1)}, u32[]{:S(2)}, u32[]{:S(2)}) %collective-permute-start.2) | collective-permute-done | bytes 589856 | tf_op jit(solution)/shard_map/ppermute | solution.py:36
  73.9 5.6 %collective-permute-done.refs_1_ = bf16[32,64,576]{2,1,0:T(8,128)(2,1)} collective-permute-done((bf16[32,64,576]{2,1,0:T(8,128)(2,1)}, bf16[32,64,576]{2,1,0:T(8,128)(2,1)}, u32[]{:S(2)}, u32[]{:S(2)}) %collective-permute-start) | collective-permute-done | bytes 2359328 | tf_op jit(solution)/shard_map/ppermute | solution.py:36
  79.5 1.7 collective-permute-start.5
  81.2 0.9 fusion.15
  82.1 0.4 fusion.5
  82.6 0.3 reduce_window_sum.11
  83.0 1.2 select_reduce_fusion.list_ref
  84.2 12.6 %collective-permute-done.5.refs_6_ = bf16[16,32,576]{2,1,0:T(8,128)(2,1)} collective-permute-done((bf16[16,32,576]{2,1,0:T(8,128)(2,1)S(1)}, bf16[16,32,576]{2,1,0:T(8,128)(2,1)}, u32[]{:S(2)}, u32[]{:S(2)}) %collective-permute-start.5) | collective-permute-done | bytes 589856 | tf_op jit(solution)/shard_map/ppermute | solution.py:36
  96.8 24.4 %attend.1 = (bf16[16,32,512]{2,1,0:T(8,128)(2,1)S(1)}, bf16[16,32,512]{2,1,0:T(8,128)(2,1)S(1)}, bf16[16,32,512]{2,1,0:T(8,128)(2,1)}, bf16[16,32,512]{2,1,0:T(8,128)(2,1)S(1)}, f32[16,128]{1,0:T(8,128)S(1)}) custom-call(s32[16]{0:T(128)S(1)} %and_select_fusion.steps_ref, s32[16,128]{1,0:T(8,128)S(1)} %select_reduce_fusion.list_ref, ...), custom_call_target="tpu_custom_call" | custom-call | flops 9126805504 | bytes 9437184 | tf_op jit(solution)/shard_map/attend/pallas_call | solution.py:166
  121.2 2.8 %collective-permute-start.9 = (bf16[16,32,512]{2,1,0:T(8,128)(2,1)S(1)}, bf16[16,32,512]{2,1,0:T(8,128)(2,1)S(1)}, u32[]{:S(2)}, u32[]{:S(2)}) collective-permute-start(bf16[16,32,512]{2,1,0:T(8,128)(2,1)S(1)} %get-tuple-element.22), channel_id=1, source_target_pairs={{0,4},{1,5},{2,6},{3,7},{4,0},{5,1},{6,2},{7,3},{8,12},{9,13},{10,... | collective-permute-start | bytes 1572872 | tf_op jit(solution)/shard_map/ppermute | solution.py:36
  124.2 12.0 %collective-permute-done.6 = f32[2,16,32]{2,1,0:T(8,128)S(1)} collective-permute-done((f32[2,16,32]{2,1,0:T(8,128)S(1)}, f32[2,16,32]{2,1,0:T(8,128)S(1)}, u32[]{:S(2)}, u32[]{:S(2)}) %collective-permute-start.6) | collective-permute-done | bytes 4128 | tf_op jit(solution)/shard_map/ppermute | solution.py:36
  136.2 12.9 %collective-permute-start.7 = (f32[1,16,32]{2,1,0:T(8,128)S(1)}, f32[1,16,32]{2,1,0:T(8,128)S(1)}, u32[]{:S(2)}, u32[]{:S(2)}) collective-permute-start(f32[1,16,32]{2,1,0:T(8,128)S(1)} %add_bitcast_fusion), channel_id=1, source_target_pairs={{0,8},{1,9},{2,10},{3,11},{4,12},{5,13},{6,14},{7,15},{8,0},{9,1},... | collective-permute-start | bytes 6152 | tf_op jit(solution)/shard_map/ppermute | solution.py:36
  149.1 0.3 collective-permute-start.8
  149.4 1.3 collective-permute-done.7
  150.8 0.3 add_convert_fusion.1
  151.2 3.1 %collective-permute-start.10 = (bf16[16,32,512]{2,1,0:T(8,128)(2,1)S(1)}, bf16[16,32,512]{2,1,0:T(8,128)(2,1)}, u32[]{:S(2)}, u32[]{:S(2)}) collective-permute-start(bf16[16,32,512]{2,1,0:T(8,128)(2,1)S(1)} %add_convert_fusion.1), channel_id=1, source_target_pairs={{0,8},{1,9},{2,10},{3,11},{4,12},{5,13},{6,14},{7,15},{8,0},{9,1},... | collective-permute-start | bytes 1572872 | tf_op jit(solution)/shard_map/ppermute | solution.py:36
  154.2 16.7 %collective-permute-done.8 = bf16[16,32,512]{2,1,0:T(8,128)(2,1)} collective-permute-done((bf16[16,32,512]{2,1,0:T(8,128)(2,1)}, bf16[16,32,512]{2,1,0:T(8,128)(2,1)}, u32[]{:S(2)}, u32[]{:S(2)}) %collective-permute-start.8) | collective-permute-done | bytes 524320 | tf_op jit(solution)/shard_map/ppermute | solution.py:36
  171.0 4.6 %collective-permute-done.10 = bf16[16,32,512]{2,1,0:T(8,128)(2,1)} collective-permute-done((bf16[16,32,512]{2,1,0:T(8,128)(2,1)S(1)}, bf16[16,32,512]{2,1,0:T(8,128)(2,1)}, u32[]{:S(2)}, u32[]{:S(2)}) %collective-permute-start.10) | collective-permute-done | bytes 524320 | tf_op jit(solution)/shard_map/ppermute | solution.py:36
  175.5 1.6 add_convert_fusion
  177.1 0.4 fusion.4
  177.7 8.3 %fusion = f32[2,2,2,2,4,7168]{5,4,3,2,1,0:T(4,128)S(1)} fusion(bf16[2,2,2,2,4,1024]{5,4,3,2,1,0:T(4,128)(2,1)S(1)} %dot_general.17, bf16[1024,7168]{1,0:T(8,128)(2,1)} %param.15), kind=kOutput, calls=%fused_computation | convolution fusion | flops 939524096 | bytes 16646144 | tf_op jit(solution)/shard_map/dot_general | solution.py:320
  185.9 0.9 fusion.8
  186.9 2.0 collective-permute-done.11
  188.9 0.2 bitcast_add_fusion
  189.2 0.9 copy-done.1
  190.2 1.8 collective-permute-start.12
  192.0 5.9 %collective-permute-done.12 = bf16[2,2,4,7168]{3,2,1,0:T(4,128)(2,1)S(1)} collective-permute-done((bf16[2,2,4,7168]{3,2,1,0:T(4,128)(2,1)S(1)}, bf16[2,2,4,7168]{3,2,1,0:T(4,128)(2,1)S(1)}, u32[]{:S(2)}, u32[]{:S(2)}) %collective-permute-start.12) | collective-permute-done | bytes 229408 | tf_op jit(solution)/shard_map/ppermute | solution.py:36
  197.9 1.1 bitcast_add_fusion.1
  199.2 4.7 %collective-permute-done.13 = bf16[2,4,7168]{2,1,0:T(4,128)(2,1)S(1)} collective-permute-done((bf16[2,4,7168]{2,1,0:T(4,128)(2,1)S(1)}, bf16[2,4,7168]{2,1,0:T(4,128)(2,1)S(1)}, u32[]{:S(2)}, u32[]{:S(2)}) %collective-permute-start.13) | collective-permute-done | bytes 114720 | tf_op jit(solution)/shard_map/ppermute | solution.py:36
  204.0 1.3 collective-permute-start.14
  205.4 4.2 %collective-permute-done.14 = bf16[4,7168]{1,0:T(4,128)(2,1)S(1)} collective-permute-done((bf16[4,7168]{1,0:T(4,128)(2,1)S(1)}, bf16[4,7168]{1,0:T(4,128)(2,1)S(1)}, u32[]{:S(2)}, u32[]{:S(2)}) %collective-permute-start.14) | collective-permute-done | bytes 57376 | tf_op jit(solution)/shard_map/ppermute | solution.py:36
  209.6 0.7 fusion.13
  (52 shorter events, 1.6 us)
Async XLA Ops:
  0.0 26.0 %copy-start = (bf16[8,128,512]{2,1,0:T(8,128)(2,1)S(1)}, bf16[8,128,512]{2,1,0:T(8,128)(2,1)}, u32[]{:S(2)}) copy-start(bf16[8,128,512]{2,1,0:T(8,128)(2,1)} %param.13) | copy-start | bytes 3145732
  3.4 2.6 %copy-start.4 = (bf16[4,1536]{1,0:T(4,128)(2,1)S(1)}, bf16[4,1536]{1,0:T(4,128)(2,1)}, u32[]{:S(2)}) copy-start(bf16[4,1536]{1,0:T(4,128)(2,1)} %param.10) | copy-start | bytes 36868
  3.4 2.8 %copy-start.6 = (s32[4,32]{1,0:T(4,128)S(1)}, s32[4,32]{1,0:T(4,128)}, u32[]{:S(2)}) copy-start(s32[4,32]{1,0:T(4,128)} %param.18) | copy-start | bytes 1540
  3.4 2.8 %copy-start.7 = (s32[4]{0:T(128)S(1)}, s32[4]{0:T(128)}, u32[]{:S(2)}) copy-start(s32[4]{0:T(128)} %param.19) | copy-start | bytes 52
  3.5 2.8 %copy-start.5 = (f32[1536]{0:T(1024)S(1)}, f32[1536]{0:T(1024)}, u32[]{:S(2)}) copy-start(f32[1536]{0:T(1024)} %param.11) | copy-start | bytes 18436
  19.7 2.3 %copy-start.3 = (bf16[64,1664]{1,0:T(8,128)(2,1)}, bf16[64,1664]{1,0:T(8,128)(2,1)S(1)}, u32[]{:S(2)}) copy-start(bf16[64,1664]{1,0:T(8,128)(2,1)S(1)} %reshape.141) | copy-start | bytes 638980
  19.8 59.7 %collective-permute-start = (bf16[32,64,576]{2,1,0:T(8,128)(2,1)}, bf16[32,64,576]{2,1,0:T(8,128)(2,1)}, u32[]{:S(2)}, u32[]{:S(2)}) collective-permute-start(bf16[32,64,576]{2,1,0:T(8,128)(2,1)} %bitcast.4.refs_0_), channel_id=1, source_target_pairs={{0,2},{1,3},{2,0},{3,1},{4,6},{5,7},{6,4},{7,5},{8,10},{9,11},{10,... | collective-permute-start | bytes 7077896 | tf_op jit(solution)/shard_map/ppermute | solution.py:36
  26.8 31.5 %collective-permute-start.1 = (bf16[16,32,576]{2,1,0:T(8,128)(2,1)S(1)}, bf16[16,32,576]{2,1,0:T(8,128)(2,1)S(1)}, u32[]{:S(2)}, u32[]{:S(2)}) collective-permute-start(bf16[16,32,576]{2,1,0:T(8,128)(2,1)S(1)} %bitcast.110), channel_id=1, source_target_pairs={{0,8},{1,9},{2,10},{3,11},{4,12},{5,13},{6,14},{7,15},{8,0},{9,1},... | collective-permute-start | bytes 1769480 | tf_op jit(solution)/shard_map/ppermute | solution.py:36
  58.3 15.6 %collective-permute-start.2 = (bf16[16,32,576]{2,1,0:T(8,128)(2,1)S(1)}, bf16[16,32,576]{2,1,0:T(8,128)(2,1)S(1)}, u32[]{:S(2)}, u32[]{:S(2)}) collective-permute-start(bf16[16,32,576]{2,1,0:T(8,128)(2,1)S(1)} %collective-permute-done.1.refs_5_), channel_id=1, source_target_pairs={{0,4},{1,5},{2,6},{3,7},{4,0},{5,1},{6,2},{7,3},{8,12},{9,13},{10,... | collective-permute-start | bytes 1769480 | tf_op jit(solution)/shard_map/ppermute | solution.py:36
  58.3 38.5 %collective-permute-start.3 = (bf16[32,64,576]{2,1,0:T(8,128)(2,1)}, bf16[32,64,576]{2,1,0:T(8,128)(2,1)}, u32[]{:S(2)}, u32[]{:S(2)}) collective-permute-start(bf16[32,64,576]{2,1,0:T(8,128)(2,1)} %bitcast.4.refs_0_), channel_id=1, source_target_pairs={{0,1},{1,0},{2,3},{3,2},{4,5},{5,4},{6,7},{7,6},{8,9},{9,8},{10,11... | collective-permute-start | bytes 7077896 | tf_op jit(solution)/shard_map/ppermute | solution.py:36
  79.5 17.3 %collective-permute-start.4 = (bf16[32,64,576]{2,1,0:T(8,128)(2,1)}, bf16[32,64,576]{2,1,0:T(8,128)(2,1)}, u32[]{:S(2)}, u32[]{:S(2)}) collective-permute-start(bf16[32,64,576]{2,1,0:T(8,128)(2,1)} %collective-permute-done.refs_1_), channel_id=1, source_target_pairs={{0,1},{1,0},{2,3},{3,2},{4,5},{5,4},{6,7},{7,6},{8,9},{9,8},{10,11... | collective-permute-start | bytes 7077896 | tf_op jit(solution)/shard_map/ppermute | solution.py:36
  79.5 17.3 %collective-permute-start.5 = (bf16[16,32,576]{2,1,0:T(8,128)(2,1)S(1)}, bf16[16,32,576]{2,1,0:T(8,128)(2,1)}, u32[]{:S(2)}, u32[]{:S(2)}) collective-permute-start(bf16[16,32,576]{2,1,0:T(8,128)(2,1)S(1)} %bitcast.111), channel_id=1, source_target_pairs={{0,4},{1,5},{2,6},{3,7},{4,0},{5,1},{6,2},{7,3},{8,12},{9,13},{10,... | collective-permute-start | bytes 1769480 | tf_op jit(solution)/shard_map/ppermute | solution.py:36
  121.1 56.0 %copy-start.2 = (bf16[8,512,128]{2,1,0:T(8,128)(2,1)S(1)}, bf16[8,512,128]{2,1,0:T(8,128)(2,1)}, u32[]{:S(2)}) copy-start(bf16[8,512,128]{2,1,0:T(8,128)(2,1)} %param.14) | copy-start | bytes 3145732
  121.2 29.6 %collective-permute-start.9 = (bf16[16,32,512]{2,1,0:T(8,128)(2,1)S(1)}, bf16[16,32,512]{2,1,0:T(8,128)(2,1)S(1)}, u32[]{:S(2)}, u32[]{:S(2)}) collective-permute-start(bf16[16,32,512]{2,1,0:T(8,128)(2,1)S(1)} %get-tuple-element.22), channel_id=1, source_target_pairs={{0,4},{1,5},{2,6},{3,7},{4,0},{5,1},{6,2},{7,3},{8,12},{9,13},{10,... | collective-permute-start | bytes 1572872 | tf_op jit(solution)/shard_map/ppermute | solution.py:36
  124.1 12.1 %collective-permute-start.6 = (f32[2,16,32]{2,1,0:T(8,128)S(1)}, f32[2,16,32]{2,1,0:T(8,128)S(1)}, u32[]{:S(2)}, u32[]{:S(2)}) collective-permute-start(f32[2,16,32]{2,1,0:T(8,128)S(1)} %pad_maximum_fusion.1), channel_id=1, source_target_pairs={{0,4},{1,5},{2,6},{3,7},{4,0},{5,1},{6,2},{7,3},{8,12},{9,13},{10,... | collective-permute-start | bytes 12296 | tf_op jit(solution)/shard_map/ppermute | solution.py:36
  136.2 14.5 %collective-permute-start.7 = (f32[1,16,32]{2,1,0:T(8,128)S(1)}, f32[1,16,32]{2,1,0:T(8,128)S(1)}, u32[]{:S(2)}, u32[]{:S(2)}) collective-permute-start(f32[1,16,32]{2,1,0:T(8,128)S(1)} %add_bitcast_fusion), channel_id=1, source_target_pairs={{0,8},{1,9},{2,10},{3,11},{4,12},{5,13},{6,14},{7,15},{8,0},{9,1},... | collective-permute-start | bytes 6152 | tf_op jit(solution)/shard_map/ppermute | solution.py:36
  149.1 21.8 %collective-permute-start.8 = (bf16[16,32,512]{2,1,0:T(8,128)(2,1)}, bf16[16,32,512]{2,1,0:T(8,128)(2,1)}, u32[]{:S(2)}, u32[]{:S(2)}) collective-permute-start(bf16[16,32,512]{2,1,0:T(8,128)(2,1)} %get-tuple-element.20), channel_id=1, source_target_pairs={{0,4},{1,5},{2,6},{3,7},{4,0},{5,1},{6,2},{7,3},{8,12},{9,13},{10,... | collective-permute-start | bytes 1572872 | tf_op jit(solution)/shard_map/ppermute | solution.py:36
  151.2 24.4 %collective-permute-start.10 = (bf16[16,32,512]{2,1,0:T(8,128)(2,1)S(1)}, bf16[16,32,512]{2,1,0:T(8,128)(2,1)}, u32[]{:S(2)}, u32[]{:S(2)}) collective-permute-start(bf16[16,32,512]{2,1,0:T(8,128)(2,1)S(1)} %add_convert_fusion.1), channel_id=1, source_target_pairs={{0,8},{1,9},{2,10},{3,11},{4,12},{5,13},{6,14},{7,15},{8,0},{9,1},... | collective-permute-start | bytes 1572872 | tf_op jit(solution)/shard_map/ppermute | solution.py:36
  186.9 2.0 collective-permute-start.11
  189.2 0.9 copy-start.1
  190.2 7.7 %collective-permute-start.12 = (bf16[2,2,4,7168]{3,2,1,0:T(4,128)(2,1)S(1)}, bf16[2,2,4,7168]{3,2,1,0:T(4,128)(2,1)S(1)}, u32[]{:S(2)}, u32[]{:S(2)}) collective-permute-start(bf16[2,2,4,7168]{3,2,1,0:T(4,128)(2,1)S(1)} %fusion.9), channel_id=1, source_target_pairs={{0,2},{1,3},{2,0},{3,1},{4,6},{5,7},{6,4},{7,5},{8,10},{9,11},{10,... | collective-permute-start | bytes 688136 | tf_op jit(solution)/shard_map/ppermute | solution.py:36
  199.1 4.9 %collective-permute-start.13 = (bf16[2,4,7168]{2,1,0:T(4,128)(2,1)S(1)}, bf16[2,4,7168]{2,1,0:T(4,128)(2,1)S(1)}, u32[]{:S(2)}, u32[]{:S(2)}) collective-permute-start(bf16[2,4,7168]{2,1,0:T(4,128)(2,1)S(1)} %fusion.12), channel_id=1, source_target_pairs={{0,4},{1,5},{2,6},{3,7},{4,0},{5,1},{6,2},{7,3},{8,12},{9,13},{10,... | collective-permute-start | bytes 344072 | tf_op jit(solution)/shard_map/ppermute | solution.py:36
  204.0 5.6 %collective-permute-start.14 = (bf16[4,7168]{1,0:T(4,128)(2,1)S(1)}, bf16[4,7168]{1,0:T(4,128)(2,1)S(1)}, u32[]{:S(2)}, u32[]{:S(2)}) collective-permute-start(bf16[4,7168]{1,0:T(4,128)(2,1)S(1)} %fusion.14), channel_id=1, source_target_pairs={{0,8},{1,9},{2,10},{3,11},{4,12},{5,13},{6,14},{7,15},{8,0},{9,1},... | collective-permute-start | bytes 172040 | tf_op jit(solution)/shard_map/ppermute | solution.py:36

commit v4 on v3

--- a/solution.py
+++ b/solution.py
@@ -11,6 +11,7 @@
 BLK = 64
 STEP = 8
 SIDE = 2
+TILES = 7
 SPLIT = 1
 
 norm_eps = 1e-06
@@ -199,6 +200,88 @@
     return value, top + jnp.log(total)
 
 
+def project_kernel(bits, tiles, rows_ref, w_ref, out_ref, weights, w_sems, *bufs):
+    n_stages = len(bits)
+    sends, recvs = bufs[:n_stages], bufs[n_stages : 2 * n_stages]
+    send_sems, recv_sems = bufs[2 * n_stages :]
+    me = lax.axis_index("ctx")
+    upper = [(me // bit) % 2 for bit in bits]
+    partner = [me + bit * (1 - 2 * up) for bit, up in zip(bits, upper)]
+    width = weights.shape[2]
+    loads = [
+        pltpu.make_async_copy(
+            w_ref.at[:, pl.ds(t * width, width)], weights.at[t], w_sems.at[t]
+        )
+        for t in range(tiles)
+    ]
+    for load in loads:
+        load.start()
+    barrier = pltpu.get_barrier_semaphore()
+    for other in partner:
+        pl.semaphore_signal(barrier, inc=1, device_id={"ctx": other})
+    pl.semaphore_wait(barrier, n_stages)
+
+    def copy_of(k, t):
+        return pltpu.make_async_remote_copy(
+            src_ref=sends[k].at[t],
+            dst_ref=recvs[k].at[t],
+            send_sem=send_sems.at[t, k],
+            recv_sem=recv_sems.at[t, k],
+            device_id={"ctx": partner[k]},
+        )
+
+    def send_half(k, t, total):
+        half = total.shape[0] // 2
+        low, high = total[:half], total[half:]
+        sends[k][t] = jnp.where(upper[k] == 1, low, high).astype(jnp.bfloat16)
+        copy_of(k, t).start()
+        return jnp.where(upper[k] == 1, high, low)
+
+    kept = {}
+    for time in range(tiles + n_stages):
+        for k in reversed(range(n_stages)):
+            t = time - 1 - k
+            if 0 <= t < tiles:
+                copy_of(k, t).wait()
+                total = kept.pop(t) + recvs[k][t].astype(jnp.float32)
+                if k + 1 < n_stages:
+                    kept[t] = send_half(k + 1, t, total)
+                else:
+                    out_ref[:, t * width : (t + 1) * width] = total.astype(jnp.bfloat16)
+        if time < tiles:
+            loads[time].wait()
+            total = jnp.dot(rows_ref[...], weights[time], preferred_element_type=jnp.float32)
+            kept[time] = send_half(0, time, total)
+
+
+def project(rows, weight, q_local, n_devices):
+    bits = [1 << i for i in range(n_devices.bit_length() - 1)]
+    depth, columns = weight.shape
+    tiles = max(t for t in range(1, TILES + 1) if columns % (t * 128) == 0)
+    width = columns // tiles
+    sizes = [rows.shape[0] >> (i + 1) for i in range(len(bits))]
+    slots = [pltpu.VMEM((tiles, size, width), jnp.bfloat16) for size in sizes]
+    vmem = pl.BlockSpec(memory_space=pltpu.VMEM)
+    return pl.pallas_call(
+        functools.partial(project_kernel, bits, tiles),
+        out_shape=jax.ShapeDtypeStruct((q_local, columns), jnp.bfloat16),
+        in_specs=[vmem, pl.BlockSpec(memory_space=pl.ANY)],
+        out_specs=vmem,
+        scratch_shapes=[
+            pltpu.VMEM((tiles, depth, width), jnp.bfloat16),
+            pltpu.SemaphoreType.DMA((tiles,)),
+            *slots,
+            *slots,
+            pltpu.SemaphoreType.DMA((tiles, len(bits))),
+            pltpu.SemaphoreType.DMA((tiles, len(bits))),
+        ],
+        compiler_params=pltpu.CompilerParams(
+            collective_id=1, has_side_effects=True, vmem_limit_bytes=48 * 2**20
+        ),
+        name="project",
+    )(rows, weight)
+
+
 def local(
     cache_bits, query_bits, q_latent, q_gain, w_uq, w_uk, w_uv, w_o, latent_cache, kv_scales, selected, counts
 ):
@@ -316,20 +399,10 @@
     head_values = jnp.einsum(
         "qhc,hcv->qhv", head_out, w_uv, preferred_element_type=jnp.float32
     ).astype(jnp.bfloat16)
-    head_values = head_values.reshape(row_count, heads_local * w_uv.shape[2])
-    result = jnp.dot(head_values, w_o, preferred_element_type=jnp.float32)
-
-    result = result.reshape((2,) * (n_devices.bit_length() - 1) + (q_local, -1))
-    axis = n_devices.bit_length() - 2
-    bit = 1
-    while bit < n_devices:
-        mine = (me // bit) % 2
-        keep = lax.dynamic_index_in_dim(result, mine, axis, keepdims=False)
-        send = lax.dynamic_index_in_dim(result, 1 - mine, axis, keepdims=False)
-        result = keep + xor_permute(send.astype(jnp.bfloat16), n_devices, bit).astype(jnp.float32)
-        axis -= 1
-        bit *= 2
-    return result.astype(jnp.bfloat16)
+    n_bits = n_devices.bit_length() - 1
+    rows = head_values.reshape((2,) * n_bits + (q_local, -1))
+    rows = rows.transpose(tuple(reversed(range(n_bits))) + (n_bits, n_bits + 1))
+    return project(rows.reshape(row_count, -1), w_o, q_local, n_devices)
 
 
 def solution(mesh):

time: 209 us -> 210 us (level)
  Pallas kernels: 36.1 us -> 69.2 us
  waiting for transfers between devices: 115 us -> 102 us
  starting transfers between devices: 28.2 us -> 18.6 us
  matrix products: 12.2 us -> 4.05 us
    pallas_call x0 -> x1, Pallas kernels: none -> 31.6 us  [project(): pl.pallas_call(functools.partial(project_kernel, bits, tiles), out_shape=...]
    ppermute x15 -> x11, waiting for transfers between devices: 115 us -> 102 us  [xor_permute(): lax.ppermute(value, 'ctx', [(i, i ^ distance) for i in range(n_devices)])]
    ppermute x15 -> x11, starting transfers between devices: 28.2 us -> 18.6 us  [xor_permute(): lax.ppermute(value, 'ctx', [(i, i ^ distance) for i in range(n_devices)])]
    dot_general x1 -> x0, matrix products: 8.28 us -> none  [local(): result = jnp.dot(head_values, w_o, preferred_element_type=jnp.float32)]
  transfers between devices with their start and end apart: 15 -> 11, of which waited for: 12 -> 8; matrix products, arithmetic and copies ran while one was open for 4% -> 4% of each run, Pallas kernels for 0% -> 0%
where the time goes in v4:
time: 210 us; the launch traced here: 211 us
  waiting for transfers between devices  102 us (49%)
  Pallas kernels  69.2 us (33%)
  starting transfers between devices  18.6 us (9%)
  other arithmetic  9.03 us (4%)
  local copies, waits for them, and re-layouts  7.5 us (4%)
  matrix products  4.05 us (2%)
    ppermute x11, waiting for transfers between devices, xor_permute(): lax.ppermute(value, 'ctx', [(i, i ^ distance) for i in range(n_devices)])  102 us
    pallas_call x1, Pallas kernels, project(): pl.pallas_call(functools.partial(project_kernel, bits, tiles), out_shape=...  31.6 us
    pallas_call x1, Pallas kernels, attend(): pl.pallas_call(functools.partial(attend_kernel, n_parts, n_chunks, first,...  25.9 us
    ppermute x11, starting transfers between devices, xor_permute(): lax.ppermute(value, 'ctx', [(i, i ^ distance) for i in range(n_devices)])  18.6 us
    pallas_call x1, Pallas kernels, gather_rows(): pl.pallas_call(functools.partial(gather_kernel, n_devices), out_shape=jax...  11.7 us
  transfers between devices with their start and end apart: 11, of which 8 were waited for; matrix products, arithmetic and copies ran while one was open for 4% of the time, Pallas kernels for 0%

profile of v4, /device:TPU:0, one launch (start us, length us, event | category | flops | bytes accessed | tf_op | source)
XLA Modules:
  0.0 210.7 jit_solution(2129667099227040286)
XLA Ops:
  0.0 0.9 fusion.11
  0.9 0.8 fusion.21
  1.7 0.8 fusion.13
  2.5 0.7 concatenate.12.own_ref
  3.2 11.7 %gather_rows.1 = bf16[16,4,1664]{2,1,0:T(4,128)(2,1)} custom-call(bf16[4,1664]{1,0:T(4,128)(2,1)} %concatenate.12.own_ref), custom_call_target="tpu_custom_call" | custom-call | tf_op jit(solution)/shard_map/gather_rows/pallas_call | solution.py:65
  14.9 1.7 reshape.139
  16.5 1.0 slice.61
  17.5 2.2 %fusion = bf16[512,2048]{1,0:T(8,128)(2,1)S(1)} fusion(bf16[576,2048]{1,0:T(8,128)(2,1)} %bitcast.91, f32[4,2048]{1,0:T(4,128)} %bitcast.95), kind=kLoop, calls=%fused_computation.1 | loop fusion | flops 3145728 | bytes 4227072 | tf_op jit(solution)/shard_map/convert_element_type | solution.py:302
  19.7 0.2 maximum_bitcast_fusion
  19.9 2.6 %copy.25 = bf16[2048,576]{1,0:T(8,128)(2,1)} copy(bf16[2048,576]{0,1:T(8,128)(2,1)S(1)} %maximum_bitcast_fusion) | data formatting | bytes 4718592 | tf_op jit(solution)/shard_map/transpose | solution.py:305
  22.4 2.2 %collective-permute-start = (bf16[32,64,576]{2,1,0:T(8,128)(2,1)}, bf16[32,64,576]{2,1,0:T(8,128)(2,1)}, u32[]{:S(2)}, u32[]{:S(2)}) collective-permute-start(bf16[32,64,576]{2,1,0:T(8,128)(2,1)} %bitcast.4.refs_0_), channel_id=1, source_target_pairs={{0,2},{1,3},{2,0},{3,1},{4,6},{5,7},{6,4},{7,5},{8,10},{9,11},{10,... | collective-permute-start | bytes 7077896 | tf_op jit(solution)/shard_map/ppermute | solution.py:37
  24.7 3.4 %fusion.6 = f32[64,1536]{1,0:T(8,128)S(1)} fusion(bf16[1536,1536]{1,0:T(8,128)(2,1)} %param.12, bf16[64,1664]{1,0:T(8,128)(2,1)} %reshape.139), kind=kOutput, calls=%fused_computation.19 | convolution fusion | flops 301989888 | bytes 5308416 | tf_op jit(solution)/shard_map/dot_general | solution.py:337
  28.0 0.2 reshape.141
  28.2 0.2 multiply_cosine_fusion
  28.4 0.1 fusion.23
  28.6 0.1 subtract_convert_fusion
  28.7 0.3 fusion.1
  29.0 0.1 pad_maximum_fusion
  29.1 0.4 copy.30
  29.5 1.9 collective-permute-start.1
  31.4 29.6 %collective-permute-done.1.refs_5_ = bf16[16,32,576]{2,1,0:T(8,128)(2,1)S(1)} collective-permute-done((bf16[16,32,576]{2,1,0:T(8,128)(2,1)S(1)}, bf16[16,32,576]{2,1,0:T(8,128)(2,1)S(1)}, u32[]{:S(2)}, u32[]{:S(2)}) %collective-permute-start.1) | collective-permute-done | bytes 589856 | tf_op jit(solution)/shard_map/ppermute | solution.py:37
  61.0 15.6 %collective-permute-done.2.refs_7_ = bf16[16,32,576]{2,1,0:T(8,128)(2,1)S(1)} collective-permute-done((bf16[16,32,576]{2,1,0:T(8,128)(2,1)S(1)}, bf16[16,32,576]{2,1,0:T(8,128)(2,1)S(1)}, u32[]{:S(2)}, u32[]{:S(2)}) %collective-permute-start.2) | collective-permute-done | bytes 589856 | tf_op jit(solution)/shard_map/ppermute | solution.py:37
  76.6 5.5 %collective-permute-done.refs_1_ = bf16[32,64,576]{2,1,0:T(8,128)(2,1)} collective-permute-done((bf16[32,64,576]{2,1,0:T(8,128)(2,1)}, bf16[32,64,576]{2,1,0:T(8,128)(2,1)}, u32[]{:S(2)}, u32[]{:S(2)}) %collective-permute-start) | collective-permute-done | bytes 2359328 | tf_op jit(solution)/shard_map/ppermute | solution.py:37
  82.1 1.7 collective-permute-start.5
  83.8 0.9 fusion.8
  84.7 0.4 fusion.3
  85.1 0.1 select_reduce_fusion.1
  85.2 0.3 reduce_window_sum.11
  85.5 0.1 convert_subtract_fusion
  85.6 1.2 select_reduce_fusion.list_ref
  86.8 12.6 %collective-permute-done.5.refs_6_ = bf16[16,32,576]{2,1,0:T(8,128)(2,1)} collective-permute-done((bf16[16,32,576]{2,1,0:T(8,128)(2,1)S(1)}, bf16[16,32,576]{2,1,0:T(8,128)(2,1)}, u32[]{:S(2)}, u32[]{:S(2)}) %collective-permute-start.5) | collective-permute-done | bytes 589856 | tf_op jit(solution)/shard_map/ppermute | solution.py:37
  99.4 25.9 %attend.1 = (bf16[16,32,512]{2,1,0:T(8,128)(2,1)S(1)}, bf16[16,32,512]{2,1,0:T(8,128)(2,1)S(1)}, bf16[16,32,512]{2,1,0:T(8,128)(2,1)S(1)}, bf16[16,32,512]{2,1,0:T(8,128)(2,1)S(1)}, f32[16,128]{1,0:T(8,128)S(1)}) custom-call(s32[16]{0:T(128)S(1)} %and_select_fusion.steps_ref, s32[16,128]{1,0:T(8,128)S(1)} %select_reduce_fusion.list_ref, ...), custom_call_target="tpu_custom_call" | custom-call | flops 9126805504 | bytes 9437184 | tf_op jit(solution)/shard_map/attend/pallas_call | solution.py:167
  125.3 10.8 %collective-permute-start.9 = (bf16[16,32,512]{2,1,0:T(8,128)(2,1)S(1)}, bf16[16,32,512]{2,1,0:T(8,128)(2,1)S(1)}, u32[]{:S(2)}, u32[]{:S(2)}) collective-permute-start(bf16[16,32,512]{2,1,0:T(8,128)(2,1)S(1)} %get-tuple-element.22), channel_id=1, source_target_pairs={{0,4},{1,5},{2,6},{3,7},{4,0},{5,1},{6,2},{7,3},{8,12},{9,13},{10,... | collective-permute-start | bytes 1572872 | tf_op jit(solution)/shard_map/ppermute | solution.py:37
  136.1 0.1 collective-permute-start.6
  136.2 12.0 %collective-permute-done.6 = f32[2,16,32]{2,1,0:T(8,128)S(1)} collective-permute-done((f32[2,16,32]{2,1,0:T(8,128)S(1)}, f32[2,16,32]{2,1,0:T(8,128)S(1)}, u32[]{:S(2)}, u32[]{:S(2)}) %collective-permute-start.6) | collective-permute-done | bytes 4128 | tf_op jit(solution)/shard_map/ppermute | solution.py:37
  148.2 0.1 add_bitcast_fusion
  148.4 1.8 collective-permute-start.8
  150.2 2.8 %collective-permute-done.7 = f32[1,16,32]{2,1,0:T(8,128)S(1)} collective-permute-done((f32[1,16,32]{2,1,0:T(8,128)S(1)}, f32[1,16,32]{2,1,0:T(8,128)S(1)}, u32[]{:S(2)}, u32[]{:S(2)}) %collective-permute-start.7) | collective-permute-done | bytes 2080 | tf_op jit(solution)/shard_map/ppermute | solution.py:37
  153.0 0.1 fusion.17
  153.1 0.3 add_convert_fusion.1
  153.4 0.1 collective-permute-start.10
  153.5 16.6 %collective-permute-done.8 = bf16[16,32,512]{2,1,0:T(8,128)(2,1)S(1)} collective-permute-done((bf16[16,32,512]{2,1,0:T(8,128)(2,1)S(1)}, bf16[16,32,512]{2,1,0:T(8,128)(2,1)S(1)}, u32[]{:S(2)}, u32[]{:S(2)}) %collective-permute-start.8) | collective-permute-done | bytes 524320 | tf_op jit(solution)/shard_map/ppermute | solution.py:37
  170.1 7.3 %collective-permute-done.10 = bf16[16,32,512]{2,1,0:T(8,128)(2,1)S(1)} collective-permute-done((bf16[16,32,512]{2,1,0:T(8,128)(2,1)S(1)}, bf16[16,32,512]{2,1,0:T(8,128)(2,1)S(1)}, u32[]{:S(2)}, u32[]{:S(2)}) %collective-permute-start.10) | collective-permute-done | bytes 524320 | tf_op jit(solution)/shard_map/ppermute | solution.py:37
  177.4 0.4 add_convert_fusion
  177.8 0.4 fusion.2
  178.2 0.1 copy.32
  178.4 31.6 %project.1 = bf16[4,7168]{1,0:T(4,128)(2,1)S(1)} custom-call(bf16[64,1024]{1,0:T(8,128)(2,1)S(1)} %reshape.145.rows_ref, bf16[1024,7168]{1,0:T(8,128)(2,1)} %w_ref.1), custom_call_target="tpu_custom_call" | custom-call | tf_op jit(solution)/shard_map/project/pallas_call | solution.py:265
  210.1 0.6 copy.47
  (27 shorter events, 0.4 us)
Async XLA Ops:
  0.0 28.7 %copy-start = (bf16[8,128,512]{2,1,0:T(8,128)(2,1)S(1)}, bf16[8,128,512]{2,1,0:T(8,128)(2,1)}, u32[]{:S(2)}) copy-start(bf16[8,128,512]{2,1,0:T(8,128)(2,1)} %param.13) | copy-start | bytes 3145732
  22.4 59.7 %collective-permute-start = (bf16[32,64,576]{2,1,0:T(8,128)(2,1)}, bf16[32,64,576]{2,1,0:T(8,128)(2,1)}, u32[]{:S(2)}, u32[]{:S(2)}) collective-permute-start(bf16[32,64,576]{2,1,0:T(8,128)(2,1)} %bitcast.4.refs_0_), channel_id=1, source_target_pairs={{0,2},{1,3},{2,0},{3,1},{4,6},{5,7},{6,4},{7,5},{8,10},{9,11},{10,... | collective-permute-start | bytes 7077896 | tf_op jit(solution)/shard_map/ppermute | solution.py:37
  29.5 31.5 %collective-permute-start.1 = (bf16[16,32,576]{2,1,0:T(8,128)(2,1)S(1)}, bf16[16,32,576]{2,1,0:T(8,128)(2,1)S(1)}, u32[]{:S(2)}, u32[]{:S(2)}) collective-permute-start(bf16[16,32,576]{2,1,0:T(8,128)(2,1)S(1)} %bitcast.87), channel_id=1, source_target_pairs={{0,8},{1,9},{2,10},{3,11},{4,12},{5,13},{6,14},{7,15},{8,0},{9,1},... | collective-permute-start | bytes 1769480 | tf_op jit(solution)/shard_map/ppermute | solution.py:37
  61.0 15.6 %collective-permute-start.2 = (bf16[16,32,576]{2,1,0:T(8,128)(2,1)S(1)}, bf16[16,32,576]{2,1,0:T(8,128)(2,1)S(1)}, u32[]{:S(2)}, u32[]{:S(2)}) collective-permute-start(bf16[16,32,576]{2,1,0:T(8,128)(2,1)S(1)} %collective-permute-done.1.refs_5_), channel_id=1, source_target_pairs={{0,4},{1,5},{2,6},{3,7},{4,0},{5,1},{6,2},{7,3},{8,12},{9,13},{10,... | collective-permute-start | bytes 1769480 | tf_op jit(solution)/shard_map/ppermute | solution.py:37
  61.0 38.4 %collective-permute-start.3 = (bf16[32,64,576]{2,1,0:T(8,128)(2,1)}, bf16[32,64,576]{2,1,0:T(8,128)(2,1)}, u32[]{:S(2)}, u32[]{:S(2)}) collective-permute-start(bf16[32,64,576]{2,1,0:T(8,128)(2,1)} %bitcast.4.refs_0_), channel_id=1, source_target_pairs={{0,1},{1,0},{2,3},{3,2},{4,5},{5,4},{6,7},{7,6},{8,9},{9,8},{10,11... | collective-permute-start | bytes 7077896 | tf_op jit(solution)/shard_map/ppermute | solution.py:37
  82.1 17.3 %collective-permute-start.4 = (bf16[32,64,576]{2,1,0:T(8,128)(2,1)}, bf16[32,64,576]{2,1,0:T(8,128)(2,1)}, u32[]{:S(2)}, u32[]{:S(2)}) collective-permute-start(bf16[32,64,576]{2,1,0:T(8,128)(2,1)} %collective-permute-done.refs_1_), channel_id=1, source_target_pairs={{0,1},{1,0},{2,3},{3,2},{4,5},{5,4},{6,7},{7,6},{8,9},{9,8},{10,11... | collective-permute-start | bytes 7077896 | tf_op jit(solution)/shard_map/ppermute | solution.py:37
  82.1 17.3 %collective-permute-start.5 = (bf16[16,32,576]{2,1,0:T(8,128)(2,1)S(1)}, bf16[16,32,576]{2,1,0:T(8,128)(2,1)}, u32[]{:S(2)}, u32[]{:S(2)}) collective-permute-start(bf16[16,32,576]{2,1,0:T(8,128)(2,1)S(1)} %bitcast.88), channel_id=1, source_target_pairs={{0,4},{1,5},{2,6},{3,7},{4,0},{5,1},{6,2},{7,3},{8,12},{9,13},{10,... | collective-permute-start | bytes 1769480 | tf_op jit(solution)/shard_map/ppermute | solution.py:37
  125.3 52.6 %copy-start.1 = (bf16[8,512,128]{2,1,0:T(8,128)(2,1)S(1)}, bf16[8,512,128]{2,1,0:T(8,128)(2,1)}, u32[]{:S(2)}) copy-start(bf16[8,512,128]{2,1,0:T(8,128)(2,1)} %param.14) | copy-start | bytes 3145732
  125.3 27.8 %collective-permute-start.9 = (bf16[16,32,512]{2,1,0:T(8,128)(2,1)S(1)}, bf16[16,32,512]{2,1,0:T(8,128)(2,1)S(1)}, u32[]{:S(2)}, u32[]{:S(2)}) collective-permute-start(bf16[16,32,512]{2,1,0:T(8,128)(2,1)S(1)} %get-tuple-element.22), channel_id=1, source_target_pairs={{0,4},{1,5},{2,6},{3,7},{4,0},{5,1},{6,2},{7,3},{8,12},{9,13},{10,... | collective-permute-start | bytes 1572872 | tf_op jit(solution)/shard_map/ppermute | solution.py:37
  136.1 12.1 %collective-permute-start.6 = (f32[2,16,32]{2,1,0:T(8,128)S(1)}, f32[2,16,32]{2,1,0:T(8,128)S(1)}, u32[]{:S(2)}, u32[]{:S(2)}) collective-permute-start(f32[2,16,32]{2,1,0:T(8,128)S(1)} %pad_maximum_fusion.1), channel_id=1, source_target_pairs={{0,4},{1,5},{2,6},{3,7},{4,0},{5,1},{6,2},{7,3},{8,12},{9,13},{10,... | collective-permute-start | bytes 12296 | tf_op jit(solution)/shard_map/ppermute | solution.py:37
  148.3 4.7 %collective-permute-start.7 = (f32[1,16,32]{2,1,0:T(8,128)S(1)}, f32[1,16,32]{2,1,0:T(8,128)S(1)}, u32[]{:S(2)}, u32[]{:S(2)}) collective-permute-start(f32[1,16,32]{2,1,0:T(8,128)S(1)} %add_bitcast_fusion), channel_id=1, source_target_pairs={{0,8},{1,9},{2,10},{3,11},{4,12},{5,13},{6,14},{7,15},{8,0},{9,1},... | collective-permute-start | bytes 6152 | tf_op jit(solution)/shard_map/ppermute | solution.py:37
  148.4 21.7 %collective-permute-start.8 = (bf16[16,32,512]{2,1,0:T(8,128)(2,1)S(1)}, bf16[16,32,512]{2,1,0:T(8,128)(2,1)S(1)}, u32[]{:S(2)}, u32[]{:S(2)}) collective-permute-start(bf16[16,32,512]{2,1,0:T(8,128)(2,1)S(1)} %get-tuple-element.20), channel_id=1, source_target_pairs={{0,4},{1,5},{2,6},{3,7},{4,0},{5,1},{6,2},{7,3},{8,12},{9,13},{10,... | collective-permute-start | bytes 1572872 | tf_op jit(solution)/shard_map/ppermute | solution.py:37
  153.4 24.0 %collective-permute-start.10 = (bf16[16,32,512]{2,1,0:T(8,128)(2,1)S(1)}, bf16[16,32,512]{2,1,0:T(8,128)(2,1)S(1)}, u32[]{:S(2)}, u32[]{:S(2)}) collective-permute-start(bf16[16,32,512]{2,1,0:T(8,128)(2,1)S(1)} %add_convert_fusion.1), channel_id=1, source_target_pairs={{0,8},{1,9},{2,10},{3,11},{4,12},{5,13},{6,14},{7,15},{8,0},{9,1},... | collective-permute-start | bytes 1572872 | tf_op jit(solution)/shard_map/ppermute | solution.py:37

commit v5 on v4

--- a/solution.py
+++ b/solution.py
@@ -12,6 +12,8 @@
 STEP = 8
 SIDE = 2
 TILES = 7
+LAG = 2
+PIECES = 2
 SPLIT = 1
 
 norm_eps = 1e-06
@@ -238,9 +240,9 @@
         return jnp.where(upper[k] == 1, high, low)
 
     kept = {}
-    for time in range(tiles + n_stages):
+    for time in range(tiles + LAG * n_stages):
         for k in reversed(range(n_stages)):
-            t = time - 1 - k
+            t = time - LAG * (k + 1)
             if 0 <= t < tiles:
                 copy_of(k, t).wait()
                 total = kept.pop(t) + recvs[k][t].astype(jnp.float32)
@@ -293,17 +295,18 @@
     q_local, top_blocks = selected.shape
     blocks_local = latent_cache.shape[0] // BLK
     tiles = kv_scales.shape[1]
-    n_parts = 2 ** len(cache_bits)
 
     cache_t = latent_cache.T
     scaled_t = (
         cache_t[:width_latent].astype(jnp.float32).reshape(tiles, width_latent // tiles, -1)
         * kv_scales.T[:, None, :]
     ).astype(jnp.bfloat16)
-    own_cache = (
-        jnp.concatenate([scaled_t.reshape(width_latent, -1), cache_t[width_latent:]], axis=0)
-        .T.reshape(blocks_local, BLK, width_row)
-    )
+    whole_t = jnp.concatenate([scaled_t.reshape(width_latent, -1), cache_t[width_latent:]], axis=0)
+    piece_blocks = blocks_local // PIECES
+    own_cache = [
+        x.T.reshape(piece_blocks, BLK, width_row) for x in jnp.split(whole_t, PIECES, axis=1)
+    ]
+
     latent_f = q_latent.astype(jnp.float32)
     normed = (
         latent_f
@@ -325,8 +328,8 @@
     gathered = gather_rows(packed, n_devices)
     gathered, own_cache = lax.optimization_barrier((gathered, own_cache))
     near_bit, far_bit = cache_bits
-    far = xor_permute(own_cache, n_devices, far_bit)
-    near = xor_permute(own_cache, n_devices, near_bit)
+    far = [xor_permute(x, n_devices, far_bit) for x in own_cache]
+    near = [xor_permute(x, n_devices, near_bit) for x in own_cache]
     parts_masks = [0, far_bit, near_bit, far_bit | near_bit]
     row_count = gathered.shape[0]
     latent_width = normed.shape[1]
@@ -353,10 +356,14 @@
         chunks = chunks + [xor_permute(c, n_devices, bit) for c in chunks]
         chunk_masks = chunk_masks + [m | bit for m in chunk_masks]
 
-    far, chunks[-1] = lax.optimization_barrier((far, chunks[-1]))
-    parts = [own_cache, far, near, xor_permute(far, n_devices, near_bit)]
-
-    n_held = n_parts * blocks_local
+    passed = []
+    for i, piece in enumerate(far):
+        j = len(chunks) - 1 if i + 1 == len(far) else 1
+        far[i], chunks[j] = lax.optimization_barrier((piece, chunks[j]))
+        passed.append(xor_permute(far[i], n_devices, near_bit))
+    parts = own_cache + far + near + passed
+
+    n_held = len(parts) * piece_blocks
     place = jnp.full_like(all_owner, -1)
     for i, mask in enumerate(parts_masks):
         place = jnp.where(all_owner == (me ^ mask), i * blocks_local + all_inner, place)

time: 210 us -> 191 us (0.910)
  waiting for transfers between devices: 102 us -> 85.2 us
  Pallas kernels: 69.2 us -> 61 us
  starting transfers between devices: 18.6 us -> 25.2 us
    ppermute x11 -> x14, waiting for transfers between devices: 102 us -> 85.2 us  [xor_permute(): lax.ppermute(value, 'ctx', [(i, i ^ distance) for i in range(n_devices)])]
    pallas_call x1, Pallas kernels: 31.6 us -> 23.3 us  [project(): pl.pallas_call(functools.partial(project_kernel, bits, tiles), out_shape=...]
    ppermute x11 -> x14, starting transfers between devices: 18.6 us -> 25.2 us  [xor_permute(): lax.ppermute(value, 'ctx', [(i, i ^ distance) for i in range(n_devices)])]
  transfers between devices with their start and end apart: 11 -> 14, of which waited for: 8 -> 7; matrix products, arithmetic and copies ran while one was open for 4% -> 4% of each run, Pallas kernels for 0% -> 0%
where the time goes in v5:
time: 191 us; the launch traced here: 192 us
  waiting for transfers between devices  85.2 us (45%)
  Pallas kernels  61 us (32%)
  starting transfers between devices  25.2 us (13%)
  other arithmetic  9.01 us (5%)
  local copies, waits for them, and re-layouts  7.08 us (4%)
  matrix products  4.05 us (2%)
    ppermute x14, waiting for transfers between devices, xor_permute(): lax.ppermute(value, 'ctx', [(i, i ^ distance) for i in range(n_devices)])  85.2 us
    pallas_call x1, Pallas kernels, attend(): pl.pallas_call(functools.partial(attend_kernel, n_parts, n_chunks, first,...  26 us
    ppermute x14, starting transfers between devices, xor_permute(): lax.ppermute(value, 'ctx', [(i, i ^ distance) for i in range(n_devices)])  25.2 us
    pallas_call x1, Pallas kernels, project(): pl.pallas_call(functools.partial(project_kernel, bits, tiles), out_shape=...  23.3 us
    pallas_call x1, Pallas kernels, gather_rows(): pl.pallas_call(functools.partial(gather_kernel, n_devices), out_shape=jax...  11.7 us
  transfers between devices with their start and end apart: 14, of which 7 were waited for; matrix products, arithmetic and copies ran while one was open for 4% of the time, Pallas kernels for 0%

profile of v5, /device:TPU:0, one launch (start us, length us, event | category | flops | bytes accessed | tf_op | source)
XLA Modules:
  0.0 191.8 jit_solution(17869819840216871504)
XLA Ops:
  0.0 0.9 fusion.14
  0.9 0.8 fusion.24
  1.7 0.8 fusion.16
  2.5 0.7 concatenate.12.own_ref
  3.2 11.7 %gather_rows.1 = bf16[16,4,1664]{2,1,0:T(4,128)(2,1)} custom-call(bf16[4,1664]{1,0:T(4,128)(2,1)} %concatenate.12.own_ref), custom_call_target="tpu_custom_call" | custom-call | tf_op jit(solution)/shard_map/gather_rows/pallas_call | solution.py:67
  14.9 1.7 reshape.142
  16.6 1.0 slice.61
  17.5 2.1 %fusion = bf16[512,2048]{1,0:T(8,128)(2,1)S(1)} fusion(bf16[576,2048]{1,0:T(8,128)(2,1)} %bitcast.97, f32[4,2048]{1,0:T(4,128)} %bitcast.101), kind=kLoop, calls=%fused_computation.1 | loop fusion | flops 3145728 | bytes 4227072 | tf_op jit(solution)/shard_map/convert_element_type | solution.py:303
  19.6 0.2 fusion.4
  19.9 1.4 copy.28
  21.3 0.7 copy.27
  22.0 2.3 %collective-permute-start = (bf16[16,64,576]{2,1,0:T(8,128)(2,1)S(1)}, bf16[16,64,576]{2,1,0:T(8,128)(2,1)}, u32[]{:S(2)}, u32[]{:S(2)}) collective-permute-start(bf16[16,64,576]{2,1,0:T(8,128)(2,1)S(1)} %bitcast.90), channel_id=1, source_target_pairs={{0,2},{1,3},{2,0},{3,1},{4,6},{5,7},{6,4},{7,5},{8,10},{9,11},{10,... | collective-permute-start | bytes 3538952 | tf_op jit(solution)/shard_map/ppermute | solution.py:39
  24.3 3.4 %fusion.9 = f32[64,1536]{1,0:T(8,128)S(1)} fusion(bf16[1536,1536]{1,0:T(8,128)(2,1)} %param.12, bf16[64,1664]{1,0:T(8,128)(2,1)} %reshape.142), kind=kOutput, calls=%fused_computation.24 | convolution fusion | flops 301989888 | bytes 5308416 | tf_op jit(solution)/shard_map/dot_general | solution.py:340
  27.7 0.2 reshape.145
  27.9 0.1 fusion.26
  28.0 0.2 multiply_cosine_fusion
  28.2 0.3 fusion.1
  28.5 0.1 subtract_convert_fusion
  28.7 0.1 pad_maximum_fusion.1
  28.8 0.4 copy.33
  29.2 1.9 collective-permute-start.1
  31.1 29.7 %collective-permute-done.1.refs_9_ = bf16[16,32,576]{2,1,0:T(8,128)(2,1)} collective-permute-done((bf16[16,32,576]{2,1,0:T(8,128)(2,1)S(1)}, bf16[16,32,576]{2,1,0:T(8,128)(2,1)}, u32[]{:S(2)}, u32[]{:S(2)}) %collective-permute-start.1) | collective-permute-done | bytes 589856 | tf_op jit(solution)/shard_map/ppermute | solution.py:39
  60.8 2.0 %collective-permute-start.8 = (bf16[16,32,576]{2,1,0:T(8,128)(2,1)S(1)}, bf16[16,32,576]{2,1,0:T(8,128)(2,1)}, u32[]{:S(2)}, u32[]{:S(2)}) collective-permute-start(bf16[16,32,576]{2,1,0:T(8,128)(2,1)S(1)} %bitcast.94), channel_id=1, source_target_pairs={{0,4},{1,5},{2,6},{3,7},{4,0},{5,1},{6,2},{7,3},{8,12},{9,13},{10,... | collective-permute-start | bytes 1769480 | tf_op jit(solution)/shard_map/ppermute | solution.py:39
  62.8 0.9 fusion.11
  63.7 0.4 fusion.6
  64.1 0.6 collective-permute-start.5
  64.6 14.0 %collective-permute-done.3.refs_11_ = bf16[16,32,576]{2,1,0:T(8,128)(2,1)} collective-permute-done((bf16[16,32,576]{2,1,0:T(8,128)(2,1)}, bf16[16,32,576]{2,1,0:T(8,128)(2,1)}, u32[]{:S(2)}, u32[]{:S(2)}) %collective-permute-start.3) | collective-permute-done | bytes 589856 | tf_op jit(solution)/shard_map/ppermute | solution.py:39
  78.7 2.9 %collective-permute-done.2.refs_3_ = bf16[16,64,576]{2,1,0:T(8,128)(2,1)} collective-permute-done((bf16[16,64,576]{2,1,0:T(8,128)(2,1)}, bf16[16,64,576]{2,1,0:T(8,128)(2,1)}, u32[]{:S(2)}, u32[]{:S(2)}) %collective-permute-start.2) | collective-permute-done | bytes 1179680 | tf_op jit(solution)/shard_map/ppermute | solution.py:39
  81.6 0.1 select_reduce_fusion.1
  81.7 0.3 reduce_window_sum.11
  82.0 0.1 convert_subtract_fusion
  82.1 1.2 select_reduce_fusion.list_ref
  83.3 7.5 %collective-permute-done.8.refs_10_ = bf16[16,32,576]{2,1,0:T(8,128)(2,1)} collective-permute-done((bf16[16,32,576]{2,1,0:T(8,128)(2,1)S(1)}, bf16[16,32,576]{2,1,0:T(8,128)(2,1)}, u32[]{:S(2)}, u32[]{:S(2)}) %collective-permute-start.8) | collective-permute-done | bytes 589856 | tf_op jit(solution)/shard_map/ppermute | solution.py:39
  90.8 26.0 %attend.1 = (bf16[16,32,512]{2,1,0:T(8,128)(2,1)S(1)}, bf16[16,32,512]{2,1,0:T(8,128)(2,1)S(1)}, bf16[16,32,512]{2,1,0:T(8,128)(2,1)S(1)}, bf16[16,32,512]{2,1,0:T(8,128)(2,1)S(1)}, f32[16,128]{1,0:T(8,128)S(1)}) custom-call(s32[16]{0:T(128)S(1)} %and_select_fusion.steps_ref, s32[16,128]{1,0:T(8,128)S(1)} %select_reduce_fusion.list_ref, ...), custom_call_target="tpu_custom_call" | custom-call | flops 4563402752 | bytes 9437184 | tf_op jit(solution)/shard_map/attend/pallas_call | solution.py:169
  116.8 0.8 collective-permute-start.12
  117.7 1.2 collective-permute-start.9
  118.9 10.3 %collective-permute-done.9 = f32[2,16,32]{2,1,0:T(8,128)S(1)} collective-permute-done((f32[2,16,32]{2,1,0:T(8,128)S(1)}, f32[2,16,32]{2,1,0:T(8,128)S(1)}, u32[]{:S(2)}, u32[]{:S(2)}) %collective-permute-start.9) | collective-permute-done | bytes 4128 | tf_op jit(solution)/shard_map/ppermute | solution.py:39
  129.2 11.6 %collective-permute-start.10 = (f32[1,16,32]{2,1,0:T(8,128)S(1)}, f32[1,16,32]{2,1,0:T(8,128)S(1)}, u32[]{:S(2)}, u32[]{:S(2)}) collective-permute-start(f32[1,16,32]{2,1,0:T(8,128)S(1)} %add_bitcast_fusion), channel_id=1, source_target_pairs={{0,8},{1,9},{2,10},{3,11},{4,12},{5,13},{6,14},{7,15},{8,0},{9,1},... | collective-permute-start | bytes 6152 | tf_op jit(solution)/shard_map/ppermute | solution.py:39
  140.9 1.7 collective-permute-start.11
  142.7 0.3 add_convert_fusion.1
  143.0 3.0 %collective-permute-start.13 = (bf16[16,32,512]{2,1,0:T(8,128)(2,1)S(1)}, bf16[16,32,512]{2,1,0:T(8,128)(2,1)S(1)}, u32[]{:S(2)}, u32[]{:S(2)}) collective-permute-start(bf16[16,32,512]{2,1,0:T(8,128)(2,1)S(1)} %add_convert_fusion.1), channel_id=1, source_target_pairs={{0,8},{1,9},{2,10},{3,11},{4,12},{5,13},{6,14},{7,15},{8,0},{9,1},... | collective-permute-start | bytes 1572872 | tf_op jit(solution)/shard_map/ppermute | solution.py:39
  146.0 15.7 %collective-permute-done.11 = bf16[16,32,512]{2,1,0:T(8,128)(2,1)S(1)} collective-permute-done((bf16[16,32,512]{2,1,0:T(8,128)(2,1)S(1)}, bf16[16,32,512]{2,1,0:T(8,128)(2,1)S(1)}, u32[]{:S(2)}, u32[]{:S(2)}) %collective-permute-start.11) | collective-permute-done | bytes 524320 | tf_op jit(solution)/shard_map/ppermute | solution.py:39
  161.7 5.1 %collective-permute-done.13 = bf16[16,32,512]{2,1,0:T(8,128)(2,1)S(1)} collective-permute-done((bf16[16,32,512]{2,1,0:T(8,128)(2,1)S(1)}, bf16[16,32,512]{2,1,0:T(8,128)(2,1)S(1)}, u32[]{:S(2)}, u32[]{:S(2)}) %collective-permute-start.13) | collective-permute-done | bytes 524320 | tf_op jit(solution)/shard_map/ppermute | solution.py:39
  166.8 0.4 add_convert_fusion
  167.2 0.4 fusion.5
  167.6 0.1 copy.35
  167.9 23.3 %project.1 = bf16[4,7168]{1,0:T(4,128)(2,1)S(1)} custom-call(bf16[64,1024]{1,0:T(8,128)(2,1)S(1)} %reshape.149.rows_ref, bf16[1024,7168]{1,0:T(8,128)(2,1)} %w_ref.1), custom_call_target="tpu_custom_call" | custom-call | tf_op jit(solution)/shard_map/project/pallas_call | solution.py:267
  191.2 0.6 copy.50
  (34 shorter events, 0.5 us)
Async XLA Ops:
  0.0 28.2 %copy-start = (bf16[8,128,512]{2,1,0:T(8,128)(2,1)S(1)}, bf16[8,128,512]{2,1,0:T(8,128)(2,1)}, u32[]{:S(2)}) copy-start(bf16[8,128,512]{2,1,0:T(8,128)(2,1)} %param.13) | copy-start | bytes 3145732
  22.0 42.0 %collective-permute-start = (bf16[16,64,576]{2,1,0:T(8,128)(2,1)S(1)}, bf16[16,64,576]{2,1,0:T(8,128)(2,1)}, u32[]{:S(2)}, u32[]{:S(2)}) collective-permute-start(bf16[16,64,576]{2,1,0:T(8,128)(2,1)S(1)} %bitcast.90), channel_id=1, source_target_pairs={{0,2},{1,3},{2,0},{3,1},{4,6},{5,7},{6,4},{7,5},{8,10},{9,11},{10,... | collective-permute-start | bytes 3538952 | tf_op jit(solution)/shard_map/ppermute | solution.py:39
  29.2 31.6 %collective-permute-start.1 = (bf16[16,32,576]{2,1,0:T(8,128)(2,1)S(1)}, bf16[16,32,576]{2,1,0:T(8,128)(2,1)}, u32[]{:S(2)}, u32[]{:S(2)}) collective-permute-start(bf16[16,32,576]{2,1,0:T(8,128)(2,1)S(1)} %bitcast.93), channel_id=1, source_target_pairs={{0,8},{1,9},{2,10},{3,11},{4,12},{5,13},{6,14},{7,15},{8,0},{9,1},... | collective-permute-start | bytes 1769480 | tf_op jit(solution)/shard_map/ppermute | solution.py:39
  31.1 50.5 %collective-permute-start.2 = (bf16[16,64,576]{2,1,0:T(8,128)(2,1)}, bf16[16,64,576]{2,1,0:T(8,128)(2,1)}, u32[]{:S(2)}, u32[]{:S(2)}) collective-permute-start(bf16[16,64,576]{2,1,0:T(8,128)(2,1)} %bitcast.6.refs_1_), channel_id=1, source_target_pairs={{0,2},{1,3},{2,0},{3,1},{4,6},{5,7},{6,4},{7,5},{8,10},{9,11},{10,... | collective-permute-start | bytes 3538952 | tf_op jit(solution)/shard_map/ppermute | solution.py:39
  60.8 17.9 %collective-permute-start.3 = (bf16[16,32,576]{2,1,0:T(8,128)(2,1)}, bf16[16,32,576]{2,1,0:T(8,128)(2,1)}, u32[]{:S(2)}, u32[]{:S(2)}) collective-permute-start(bf16[16,32,576]{2,1,0:T(8,128)(2,1)} %collective-permute-done.1.refs_9_), channel_id=1, source_target_pairs={{0,4},{1,5},{2,6},{3,7},{4,0},{5,1},{6,2},{7,3},{8,12},{9,13},{10,... | collective-permute-start | bytes 1769480 | tf_op jit(solution)/shard_map/ppermute | solution.py:39
  60.8 30.0 %collective-permute-start.8 = (bf16[16,32,576]{2,1,0:T(8,128)(2,1)S(1)}, bf16[16,32,576]{2,1,0:T(8,128)(2,1)}, u32[]{:S(2)}, u32[]{:S(2)}) collective-permute-start(bf16[16,32,576]{2,1,0:T(8,128)(2,1)S(1)} %bitcast.94), channel_id=1, source_target_pairs={{0,4},{1,5},{2,6},{3,7},{4,0},{5,1},{6,2},{7,3},{8,12},{9,13},{10,... | collective-permute-start | bytes 1769480 | tf_op jit(solution)/shard_map/ppermute | solution.py:39
  62.8 28.0 %collective-permute-start.4 = (bf16[16,64,576]{2,1,0:T(8,128)(2,1)S(1)}, bf16[16,64,576]{2,1,0:T(8,128)(2,1)}, u32[]{:S(2)}, u32[]{:S(2)}) collective-permute-start(bf16[16,64,576]{2,1,0:T(8,128)(2,1)S(1)} %bitcast.91), channel_id=1, source_target_pairs={{0,1},{1,0},{2,3},{3,2},{4,5},{5,4},{6,7},{7,6},{8,9},{9,8},{10,11... | collective-permute-start | bytes 3538952 | tf_op jit(solution)/shard_map/ppermute | solution.py:39
  64.1 26.7 %collective-permute-start.5 = (bf16[16,64,576]{2,1,0:T(8,128)(2,1)}, bf16[16,64,576]{2,1,0:T(8,128)(2,1)}, u32[]{:S(2)}, u32[]{:S(2)}) collective-permute-start(bf16[16,64,576]{2,1,0:T(8,128)(2,1)} %bitcast.6.refs_1_), channel_id=1, source_target_pairs={{0,1},{1,0},{2,3},{3,2},{4,5},{5,4},{6,7},{7,6},{8,9},{9,8},{10,11... | collective-permute-start | bytes 3538952 | tf_op jit(solution)/shard_map/ppermute | solution.py:39
  78.7 12.1 %collective-permute-start.6 = (bf16[16,64,576]{2,1,0:T(8,128)(2,1)}, bf16[16,64,576]{2,1,0:T(8,128)(2,1)}, u32[]{:S(2)}, u32[]{:S(2)}) collective-permute-start(bf16[16,64,576]{2,1,0:T(8,128)(2,1)} %collective-permute-done.refs_2_), channel_id=1, source_target_pairs={{0,1},{1,0},{2,3},{3,2},{4,5},{5,4},{6,7},{7,6},{8,9},{9,8},{10,11... | collective-permute-start | bytes 3538952 | tf_op jit(solution)/shard_map/ppermute | solution.py:39
  81.6 9.2 %collective-permute-start.7 = (bf16[16,64,576]{2,1,0:T(8,128)(2,1)}, bf16[16,64,576]{2,1,0:T(8,128)(2,1)}, u32[]{:S(2)}, u32[]{:S(2)}) collective-permute-start(bf16[16,64,576]{2,1,0:T(8,128)(2,1)} %collective-permute-done.2.refs_3_), channel_id=1, source_target_pairs={{0,1},{1,0},{2,3},{3,2},{4,5},{5,4},{6,7},{7,6},{8,9},{9,8},{10,11... | collective-permute-start | bytes 3538952 | tf_op jit(solution)/shard_map/ppermute | solution.py:39
  116.8 50.5 %copy-start.1 = (bf16[8,512,128]{2,1,0:T(8,128)(2,1)S(1)}, bf16[8,512,128]{2,1,0:T(8,128)(2,1)}, u32[]{:S(2)}) copy-start(bf16[8,512,128]{2,1,0:T(8,128)(2,1)} %param.14) | copy-start | bytes 3145732
  116.8 25.9 %collective-permute-start.12 = (bf16[16,32,512]{2,1,0:T(8,128)(2,1)S(1)}, bf16[16,32,512]{2,1,0:T(8,128)(2,1)S(1)}, u32[]{:S(2)}, u32[]{:S(2)}) collective-permute-start(bf16[16,32,512]{2,1,0:T(8,128)(2,1)S(1)} %get-tuple-element.28), channel_id=1, source_target_pairs={{0,4},{1,5},{2,6},{3,7},{4,0},{5,1},{6,2},{7,3},{8,12},{9,13},{10,... | collective-permute-start | bytes 1572872 | tf_op jit(solution)/shard_map/ppermute | solution.py:39
  117.7 11.5 %collective-permute-start.9 = (f32[2,16,32]{2,1,0:T(8,128)S(1)}, f32[2,16,32]{2,1,0:T(8,128)S(1)}, u32[]{:S(2)}, u32[]{:S(2)}) collective-permute-start(f32[2,16,32]{2,1,0:T(8,128)S(1)} %pad_maximum_fusion.2), channel_id=1, source_target_pairs={{0,4},{1,5},{2,6},{3,7},{4,0},{5,1},{6,2},{7,3},{8,12},{9,13},{10,... | collective-permute-start | bytes 12296 | tf_op jit(solution)/shard_map/ppermute | solution.py:39
  129.2 13.4 %collective-permute-start.10 = (f32[1,16,32]{2,1,0:T(8,128)S(1)}, f32[1,16,32]{2,1,0:T(8,128)S(1)}, u32[]{:S(2)}, u32[]{:S(2)}) collective-permute-start(f32[1,16,32]{2,1,0:T(8,128)S(1)} %add_bitcast_fusion), channel_id=1, source_target_pairs={{0,8},{1,9},{2,10},{3,11},{4,12},{5,13},{6,14},{7,15},{8,0},{9,1},... | collective-permute-start | bytes 6152 | tf_op jit(solution)/shard_map/ppermute | solution.py:39
  140.9 20.8 %collective-permute-start.11 = (bf16[16,32,512]{2,1,0:T(8,128)(2,1)S(1)}, bf16[16,32,512]{2,1,0:T(8,128)(2,1)S(1)}, u32[]{:S(2)}, u32[]{:S(2)}) collective-permute-start(bf16[16,32,512]{2,1,0:T(8,128)(2,1)S(1)} %get-tuple-element.26), channel_id=1, source_target_pairs={{0,4},{1,5},{2,6},{3,7},{4,0},{5,1},{6,2},{7,3},{8,12},{9,13},{10,... | collective-permute-start | bytes 1572872 | tf_op jit(solution)/shard_map/ppermute | solution.py:39
  143.0 23.8 %collective-permute-start.13 = (bf16[16,32,512]{2,1,0:T(8,128)(2,1)S(1)}, bf16[16,32,512]{2,1,0:T(8,128)(2,1)S(1)}, u32[]{:S(2)}, u32[]{:S(2)}) collective-permute-start(bf16[16,32,512]{2,1,0:T(8,128)(2,1)S(1)} %add_convert_fusion.1), channel_id=1, source_target_pairs={{0,8},{1,9},{2,10},{3,11},{4,12},{5,13},{6,14},{7,15},{8,0},{9,1},... | collective-permute-start | bytes 1572872 | tf_op jit(solution)/shard_map/ppermute | solution.py:39
